TPU v7x, 128 devices: a whole 4x4x4 slice. The times are simulated.
128 devices in a mesh: req: 32 (over x, y, core), tp: 4 (over z).
Axes of the slice: x: 4, y: 4, z: 4, core: 2. Of those that a mesh axis runs over, the one named last changes fastest.
Arguments:
- hidden_in: bfloat16 [32768, 2048], P('req'), may hold values from -6 to 6
- norm_gain: bfloat16 [2048], replicated, may hold values from 0.099609375 to 1.8984375
- w_query: bfloat16 [2048, 1280], P(None, 'tp'), may hold values from -0.125 to 0.125
- key_value_weight: bfloat16 [2048, 640], replicated, may hold values from -0.3125 to 0.3125
- w_out: bfloat16 [1280, 2048], replicated, may hold values from -0.625 to 0.625
- prior_cache: bfloat16 [32, 7168, 640], P('req'), may hold values from -52 to 52
- cache_len: int32 [32], P('req'), may hold values from 1 to 7168, 114688 in all
- group_len: int32 [32], P('req'), may hold values from 1 to 1024, 16384 in all
- page_map: int32 [32, 128], P('req'), may hold values from 0 to 127, each once within a row
Outputs:
- hidden_out: bfloat16 [32768, 2048], P(('req', 'tp'))
- decode_kv: bfloat16 [128, 32, 64, 640], P(('req', 'tp'))
Inputs may be any that keep to these rules, and one draw needn't show every extreme that they name: `page_map`: each row names every device index once.
All inputs are finite; a program needn't handle non-finite values. No bound on the sum of `cache_len` or of `group_len` on one device may be relied on, other than what follows from the above.
Results may differ from a plain program's by a relative error of at most 0.014.
The roundings to bfloat16 on the way count: a program that leaves them out, or rounds other values in their place, can miss the bound.
Values may be sent and summed in bfloat16 or wider, within the bound.
No kernel may reach another device: no remote copies, remote signals or barrier semaphores. Data moves between devices by JAX's collectives and lax.ppermute only.
A program may use at most 128 MiB of HBM per device.

v0:
```python
import jax
import jax.numpy as jnp
from jax import lax
from jax.sharding import PartitionSpec as P

QUERY_HEAD_COUNT = 20
KEY_VALUE_HEADS = 5
HEAD_SIZE = 64
NEW_TOKEN_SLOTS = 1024
PRIOR_SLOTS = 7168
KEYS_PER_BLOCK = 512


def rotation_table(values, token_positions, heads):
    half_size = HEAD_SIZE // 2
    frequency = 10000.0 ** (-(jnp.arange(half_size, dtype=jnp.float32) * 2.0 / HEAD_SIZE))
    angles = token_positions.astype(jnp.float32)[:, None] * frequency[None, :]
    cosine = jnp.cos(angles)[:, None, :]
    sine_part = jnp.sin(angles)[:, None, :]
    shaped = values.reshape(values.shape[0], heads, HEAD_SIZE)
    first_half = shaped[..., :half_size]
    second_half = shaped[..., half_size:]
    turned = jnp.concatenate(
        [
            first_half * cosine - second_half * sine_part,
            second_half * cosine + first_half * sine_part,
        ],
        axis=-1,
    )
    return turned.reshape(values.shape)


def project_keyval(unrotated_input, token_positions):
    key_span_width = KEY_VALUE_HEADS * HEAD_SIZE
    return jnp.concatenate(
        [
            rotation_table(unrotated_input[:, :key_span_width], token_positions, KEY_VALUE_HEADS),
            unrotated_input[:, key_span_width:],
        ],
        axis=1,
    ).astype(jnp.bfloat16)


def flash_local(carry, start, query_heads, context_output, key_value_index, cached, fresh, row_ids):
    top_score, denom_sum, weighted = carry
    key_span_width = KEY_VALUE_HEADS * HEAD_SIZE
    block_current = lax.dynamic_slice_in_dim(context_output, start, KEYS_PER_BLOCK, 0)
    key_tile = jnp.take(
        block_current[:, :key_span_width].reshape(KEYS_PER_BLOCK, KEY_VALUE_HEADS, HEAD_SIZE),
        key_value_index,
        axis=1,
    )
    value_tile = jnp.take(
        block_current[:, key_span_width:].reshape(KEYS_PER_BLOCK, KEY_VALUE_HEADS, HEAD_SIZE),
        key_value_index,
        axis=1,
    )
    columns = start + jnp.arange(KEYS_PER_BLOCK, dtype=jnp.int32)
    later = columns[None, :] - PRIOR_SLOTS
    allowed = (columns[None, :] < cached) | (later >= 0) & (later <= row_ids[:, None]) & (
        later < fresh
    )
    scores = jnp.einsum(
        "qhd,khd->qhk", query_heads, key_tile, preferred_element_type=jnp.float32
    ) * HEAD_SIZE ** (-0.5)
    scores = jnp.where(allowed[:, None, :], scores, -1e30)
    new_top = jnp.maximum(top_score, jnp.max(scores, axis=-1))
    rescale = jnp.exp(top_score - new_top)
    chances = jnp.where(allowed[:, None, :], jnp.exp(scores - new_top[..., None]), 0.0).astype(
        jnp.bfloat16
    )
    denom_sum = denom_sum * rescale + jnp.sum(chances.astype(jnp.float32), axis=-1)
    weighted = weighted * rescale[..., None] + jnp.einsum(
        "qhk,khd->qhd", chances, value_tile, preferred_element_type=jnp.float32
    )
    return (new_top, denom_sum, weighted)


def shards(
    hidden_in,
    norm_gain,
    w_query,
    key_value_weight,
    w_out,
    prior_cache,
    cache_len,
    group_len,
    page_map,
):
    tensor_parallel_rank = lax.axis_index("tp")
    tp_count = lax.axis_size("tp")
    req_count = lax.axis_size("req")
    row_total = hidden_in.shape[0]
    span = row_total // tp_count
    requests_here = prior_cache.shape[0]
    key_span_width = KEY_VALUE_HEADS * HEAD_SIZE
    local_heads = w_query.shape[1] // HEAD_SIZE
    context_rows = PRIOR_SLOTS + NEW_TOKEN_SLOTS
    block_rows = context_rows // page_map.shape[1]
    hidden = hidden_in.astype(jnp.float32)
    normed = (
        hidden
        * lax.rsqrt(jnp.mean(hidden * hidden, axis=-1, keepdims=True) + 1e-05)
        * norm_gain.astype(jnp.float32)
    ).astype(jnp.bfloat16)
    offsets = jnp.arange(NEW_TOKEN_SLOTS, dtype=jnp.int32)
    token_positions = (cache_len[:, None] + offsets[None, :]).reshape(-1)
    queries = rotation_table(
        jnp.dot(normed, w_query, preferred_element_type=jnp.float32), token_positions, local_heads
    ).astype(jnp.bfloat16)
    key_value_rows = project_keyval(
        jnp.dot(normed, key_value_weight, preferred_element_type=jnp.float32), token_positions
    )
    key_value_index = (
        tensor_parallel_rank * local_heads + jnp.arange(local_heads, dtype=jnp.int32)
    ) // (QUERY_HEAD_COUNT // KEY_VALUE_HEADS)
    targets = jnp.arange(req_count, dtype=jnp.int32) * tp_count + tensor_parallel_rank
    zero = jnp.zeros((), jnp.bfloat16)
    cached = cache_len[0]
    fresh = group_len[0]
    old_part = jnp.where(
        (jnp.arange(PRIOR_SLOTS, dtype=jnp.int32) < cached)[:, None], prior_cache[0], zero
    )
    new_part = jnp.where((offsets < fresh)[:, None], key_value_rows, zero)
    context_output = jnp.concatenate([old_part, new_part], axis=0)
    query_heads = queries.reshape(NEW_TOKEN_SLOTS, local_heads, HEAD_SIZE)
    initial = (
        jnp.full((NEW_TOKEN_SLOTS, local_heads), -1e30, jnp.float32),
        jnp.zeros((NEW_TOKEN_SLOTS, local_heads), jnp.float32),
        jnp.zeros((NEW_TOKEN_SLOTS, local_heads, HEAD_SIZE), jnp.float32),
    )

    def advance(
        counter,
        carry,
        query_heads=query_heads,
        context_output=context_output,
        cached=cached,
        fresh=fresh,
    ):
        return flash_local(
            carry,
            counter * KEYS_PER_BLOCK,
            query_heads,
            context_output,
            key_value_index,
            cached,
            fresh,
            offsets,
        )

    carry = lax.fori_loop(0, context_rows // KEYS_PER_BLOCK, advance, initial)
    attended = (
        (carry[2] / carry[1][..., None])
        .astype(jnp.bfloat16)
        .reshape(NEW_TOKEN_SLOTS, local_heads * HEAD_SIZE)
    )
    inverse = jnp.argsort(page_map[0])
    picks = inverse[targets]
    outgoing = [context_output.reshape(-1, block_rows, 2 * key_span_width)[picks]]
    live_rows = (offsets[None, :] < group_len[:, None]).reshape(-1)
    live_part = lax.dynamic_slice_in_dim(live_rows, tensor_parallel_rank * span, span, 0)
    hidden_part = lax.dynamic_slice_in_dim(hidden, tensor_parallel_rank * span, span, 0)
    own_weights = lax.dynamic_slice_in_dim(
        w_out, tensor_parallel_rank * local_heads * HEAD_SIZE, local_heads * HEAD_SIZE, 0
    )
    mixed = lax.psum_scatter(
        jnp.dot(attended, own_weights, preferred_element_type=jnp.float32).astype(jnp.bfloat16),
        "tp",
        scatter_dimension=0,
        tiled=True,
    ).astype(jnp.float32)
    hidden_out = jnp.where(live_part[:, None], hidden_part + mixed, 0.0).astype(jnp.bfloat16)
    shipment = jnp.stack(outgoing, axis=1)
    received = lax.all_to_all(shipment, "req", split_axis=0, concat_axis=0, tiled=True)
    decode_kv = received.reshape(1, req_count * requests_here, block_rows, 2 * key_span_width)
    return (hidden_out, decode_kv)


def solution(mesh):
    placed = (
        P("req", None),
        P(),
        P(None, "tp"),
        P(),
        P(),
        P("req", None, None),
        P("req"),
        P("req"),
        P("req", None),
    )
    return jax.shard_map(
        shards,
        mesh=mesh,
        in_specs=placed,
        out_specs=(P(("req", "tp"), None), P(("req", "tp"), None, None, None)),
        check_vma=False,
    )
```

profile of v0, /device:TPU:24, one launch (start us, length us, event | category | flops | bytes accessed | tf_op | source)
XLA Modules:
  0.0 520.1 jit_solution(14654515766340460179)
XLA Ops:
  26.2 6.8 %bitcast_select_fusion.1 = bf16[7168,640]{1,0:T(8,128)(2,1)S(1)} fusion(bf16[1,7168,640]{2,1,0:T(8,128)(2,1)} %param.18, pred[7168]{0:T(1024)(128)(4,1)S(1)} %iota_compare_fusion.1), kind=kLoop, calls=%fused_computation.46 | loop fusion | flops 4587520 | bytes 18357248 | tf_op jit(solution)/shard_map/jit(_where)/select_n | solution.py:121
  37.6 411.6 %while.20 = (s32[]{:T(128)}, f32[1024,5]{0,1:T(8,128)S(1)}, f32[1024,5]{0,1:T(8,128)S(1)}, f32[1024,5,64]{0,2,1:T(8,128)}, s32[]{:T(128)}, /*index=5*/s32[]{:T(1...) while((s32[]{:T(128)}, f32[1024,5]{0,1:T(8,128)S(1)}, ...), condition=%wide.region_4.6_spmd.clone, body=%wide.region_1.5_spmd.clone.sunk | while | flops 713849600 | bytes 41758032 | solution.py:152
  47.7 6.5 %convert_reduce_fusion.2 = f32[1024,5]{0,1:T(8,128)S(1)} fusion(f32[1024,5]{0,1:T(8,128)S(1)} %select_maximum_fusion.2, f32[5,512,1024]{2,1,0:T(8,128)} %get-tuple-element.406, pred[1024,512]{0,1:T(8,128)(4,1)S(1)} %fusion.51), kind=kLoop, calls=%fused_computation.7.clone.1 | loop fusion | flops 18344960 | bytes 11051008 | tf_op jit(solution)/shard_map/while/body/eval_jaxpr/reduce_sum | solution.py:72
  55.0 8.0 %fusion.55 = f32[1024,5,64]{0,2,1:T(8,128)} fusion(f32[1024,5,64]{0,2,1:T(8,128)} %get-tuple-element.427, f32[1024,5]{0,1:T(8,128)S(1)} %get-tuple-element.408, pred[]{:T(512)S(6)} %compare.9, bf16[5,512,64]{1,2,0:T(8,128)(2,1)S(1)} %gather_fusion.1, pred[5]{0:T(512)(128)(4,1)S(1)} %compare_and_fusion.2, f32[5,512,1024]{2,1,0:T(8,128)} %get-tuple-element.406, ...), kind=kOutput, calls=%fused_computation.15.clone.1 | convolution fusion | flops 349798400 | bytes 14000134 | tf_op jit(solution)/shard_map/while/body/eval_jaxpr/qhk,khd->qhd/dot_general | solution.py:73
  73.1 6.5 %convert_reduce_fusion.2 = f32[1024,5]{0,1:T(8,128)S(1)} fusion(f32[1024,5]{0,1:T(8,128)S(1)} %select_maximum_fusion.2, f32[5,512,1024]{2,1,0:T(8,128)} %get-tuple-element.406, pred[1024,512]{0,1:T(8,128)(4,1)S(1)} %fusion.51), kind=kLoop, calls=%fused_computation.7.clone.1 | loop fusion | flops 18344960 | bytes 11051008 | tf_op jit(solution)/shard_map/while/body/eval_jaxpr/reduce_sum | solution.py:72
  80.4 8.3 %fusion.55 = f32[1024,5,64]{0,2,1:T(8,128)} fusion(f32[1024,5,64]{0,2,1:T(8,128)} %get-tuple-element.427, f32[1024,5]{0,1:T(8,128)S(1)} %get-tuple-element.408, pred[]{:T(512)S(6)} %compare.9, bf16[5,512,64]{1,2,0:T(8,128)(2,1)S(1)} %gather_fusion.1, pred[5]{0:T(512)(128)(4,1)S(1)} %compare_and_fusion.2, f32[5,512,1024]{2,1,0:T(8,128)} %get-tuple-element.406, ...), kind=kOutput, calls=%fused_computation.15.clone.1 | convolution fusion | flops 349798400 | bytes 14000134 | tf_op jit(solution)/shard_map/while/body/eval_jaxpr/qhk,khd->qhd/dot_general | solution.py:73
  98.9 6.5 %convert_reduce_fusion.2 = f32[1024,5]{0,1:T(8,128)S(1)} fusion(f32[1024,5]{0,1:T(8,128)S(1)} %select_maximum_fusion.2, f32[5,512,1024]{2,1,0:T(8,128)} %get-tuple-element.406, pred[1024,512]{0,1:T(8,128)(4,1)S(1)} %fusion.51), kind=kLoop, calls=%fused_computation.7.clone.1 | loop fusion | flops 18344960 | bytes 11051008 | tf_op jit(solution)/shard_map/while/body/eval_jaxpr/reduce_sum | solution.py:72
  106.2 8.3 %fusion.55 = f32[1024,5,64]{0,2,1:T(8,128)} fusion(f32[1024,5,64]{0,2,1:T(8,128)} %get-tuple-element.427, f32[1024,5]{0,1:T(8,128)S(1)} %get-tuple-element.408, pred[]{:T(512)S(6)} %compare.9, bf16[5,512,64]{1,2,0:T(8,128)(2,1)S(1)} %gather_fusion.1, pred[5]{0:T(512)(128)(4,1)S(1)} %compare_and_fusion.2, f32[5,512,1024]{2,1,0:T(8,128)} %get-tuple-element.406, ...), kind=kOutput, calls=%fused_computation.15.clone.1 | convolution fusion | flops 349798400 | bytes 14000134 | tf_op jit(solution)/shard_map/while/body/eval_jaxpr/qhk,khd->qhd/dot_general | solution.py:73
  124.6 6.5 %convert_reduce_fusion.2 = f32[1024,5]{0,1:T(8,128)S(1)} fusion(f32[1024,5]{0,1:T(8,128)S(1)} %select_maximum_fusion.2, f32[5,512,1024]{2,1,0:T(8,128)} %get-tuple-element.406, pred[1024,512]{0,1:T(8,128)(4,1)S(1)} %fusion.51), kind=kLoop, calls=%fused_computation.7.clone.1 | loop fusion | flops 18344960 | bytes 11051008 | tf_op jit(solution)/shard_map/while/body/eval_jaxpr/reduce_sum | solution.py:72
  131.9 8.3 %fusion.55 = f32[1024,5,64]{0,2,1:T(8,128)} fusion(f32[1024,5,64]{0,2,1:T(8,128)} %get-tuple-element.427, f32[1024,5]{0,1:T(8,128)S(1)} %get-tuple-element.408, pred[]{:T(512)S(6)} %compare.9, bf16[5,512,64]{1,2,0:T(8,128)(2,1)S(1)} %gather_fusion.1, pred[5]{0:T(512)(128)(4,1)S(1)} %compare_and_fusion.2, f32[5,512,1024]{2,1,0:T(8,128)} %get-tuple-element.406, ...), kind=kOutput, calls=%fused_computation.15.clone.1 | convolution fusion | flops 349798400 | bytes 14000134 | tf_op jit(solution)/shard_map/while/body/eval_jaxpr/qhk,khd->qhd/dot_general | solution.py:73
  150.4 6.5 %convert_reduce_fusion.2 = f32[1024,5]{0,1:T(8,128)S(1)} fusion(f32[1024,5]{0,1:T(8,128)S(1)} %select_maximum_fusion.2, f32[5,512,1024]{2,1,0:T(8,128)} %get-tuple-element.406, pred[1024,512]{0,1:T(8,128)(4,1)S(1)} %fusion.51), kind=kLoop, calls=%fused_computation.7.clone.1 | loop fusion | flops 18344960 | bytes 11051008 | tf_op jit(solution)/shard_map/while/body/eval_jaxpr/reduce_sum | solution.py:72
  157.7 8.3 %fusion.55 = f32[1024,5,64]{0,2,1:T(8,128)} fusion(f32[1024,5,64]{0,2,1:T(8,128)} %get-tuple-element.427, f32[1024,5]{0,1:T(8,128)S(1)} %get-tuple-element.408, pred[]{:T(512)S(6)} %compare.9, bf16[5,512,64]{1,2,0:T(8,128)(2,1)S(1)} %gather_fusion.1, pred[5]{0:T(512)(128)(4,1)S(1)} %compare_and_fusion.2, f32[5,512,1024]{2,1,0:T(8,128)} %get-tuple-element.406, ...), kind=kOutput, calls=%fused_computation.15.clone.1 | convolution fusion | flops 349798400 | bytes 14000134 | tf_op jit(solution)/shard_map/while/body/eval_jaxpr/qhk,khd->qhd/dot_general | solution.py:73
  176.1 6.5 %convert_reduce_fusion.2 = f32[1024,5]{0,1:T(8,128)S(1)} fusion(f32[1024,5]{0,1:T(8,128)S(1)} %select_maximum_fusion.2, f32[5,512,1024]{2,1,0:T(8,128)} %get-tuple-element.406, pred[1024,512]{0,1:T(8,128)(4,1)S(1)} %fusion.51), kind=kLoop, calls=%fused_computation.7.clone.1 | loop fusion | flops 18344960 | bytes 11051008 | tf_op jit(solution)/shard_map/while/body/eval_jaxpr/reduce_sum | solution.py:72
  183.4 8.3 %fusion.55 = f32[1024,5,64]{0,2,1:T(8,128)} fusion(f32[1024,5,64]{0,2,1:T(8,128)} %get-tuple-element.427, f32[1024,5]{0,1:T(8,128)S(1)} %get-tuple-element.408, pred[]{:T(512)S(6)} %compare.9, bf16[5,512,64]{1,2,0:T(8,128)(2,1)S(1)} %gather_fusion.1, pred[5]{0:T(512)(128)(4,1)S(1)} %compare_and_fusion.2, f32[5,512,1024]{2,1,0:T(8,128)} %get-tuple-element.406, ...), kind=kOutput, calls=%fused_computation.15.clone.1 | convolution fusion | flops 349798400 | bytes 14000134 | tf_op jit(solution)/shard_map/while/body/eval_jaxpr/qhk,khd->qhd/dot_general | solution.py:73
  201.9 6.5 %convert_reduce_fusion.2 = f32[1024,5]{0,1:T(8,128)S(1)} fusion(f32[1024,5]{0,1:T(8,128)S(1)} %select_maximum_fusion.2, f32[5,512,1024]{2,1,0:T(8,128)} %get-tuple-element.406, pred[1024,512]{0,1:T(8,128)(4,1)S(1)} %fusion.51), kind=kLoop, calls=%fused_computation.7.clone.1 | loop fusion | flops 18344960 | bytes 11051008 | tf_op jit(solution)/shard_map/while/body/eval_jaxpr/reduce_sum | solution.py:72
  209.2 8.3 %fusion.55 = f32[1024,5,64]{0,2,1:T(8,128)} fusion(f32[1024,5,64]{0,2,1:T(8,128)} %get-tuple-element.427, f32[1024,5]{0,1:T(8,128)S(1)} %get-tuple-element.408, pred[]{:T(512)S(6)} %compare.9, bf16[5,512,64]{1,2,0:T(8,128)(2,1)S(1)} %gather_fusion.1, pred[5]{0:T(512)(128)(4,1)S(1)} %compare_and_fusion.2, f32[5,512,1024]{2,1,0:T(8,128)} %get-tuple-element.406, ...), kind=kOutput, calls=%fused_computation.15.clone.1 | convolution fusion | flops 349798400 | bytes 14000134 | tf_op jit(solution)/shard_map/while/body/eval_jaxpr/qhk,khd->qhd/dot_general | solution.py:73
  227.6 6.5 %convert_reduce_fusion.2 = f32[1024,5]{0,1:T(8,128)S(1)} fusion(f32[1024,5]{0,1:T(8,128)S(1)} %select_maximum_fusion.2, f32[5,512,1024]{2,1,0:T(8,128)} %get-tuple-element.406, pred[1024,512]{0,1:T(8,128)(4,1)S(1)} %fusion.51), kind=kLoop, calls=%fused_computation.7.clone.1 | loop fusion | flops 18344960 | bytes 11051008 | tf_op jit(solution)/shard_map/while/body/eval_jaxpr/reduce_sum | solution.py:72
  234.9 8.3 %fusion.55 = f32[1024,5,64]{0,2,1:T(8,128)} fusion(f32[1024,5,64]{0,2,1:T(8,128)} %get-tuple-element.427, f32[1024,5]{0,1:T(8,128)S(1)} %get-tuple-element.408, pred[]{:T(512)S(6)} %compare.9, bf16[5,512,64]{1,2,0:T(8,128)(2,1)S(1)} %gather_fusion.1, pred[5]{0:T(512)(128)(4,1)S(1)} %compare_and_fusion.2, f32[5,512,1024]{2,1,0:T(8,128)} %get-tuple-element.406, ...), kind=kOutput, calls=%fused_computation.15.clone.1 | convolution fusion | flops 349798400 | bytes 14000134 | tf_op jit(solution)/shard_map/while/body/eval_jaxpr/qhk,khd->qhd/dot_general | solution.py:73
  253.4 6.5 %convert_reduce_fusion.2 = f32[1024,5]{0,1:T(8,128)S(1)} fusion(f32[1024,5]{0,1:T(8,128)S(1)} %select_maximum_fusion.2, f32[5,512,1024]{2,1,0:T(8,128)} %get-tuple-element.406, pred[1024,512]{0,1:T(8,128)(4,1)S(1)} %fusion.51), kind=kLoop, calls=%fused_computation.7.clone.1 | loop fusion | flops 18344960 | bytes 11051008 | tf_op jit(solution)/shard_map/while/body/eval_jaxpr/reduce_sum | solution.py:72
  260.7 8.3 %fusion.55 = f32[1024,5,64]{0,2,1:T(8,128)} fusion(f32[1024,5,64]{0,2,1:T(8,128)} %get-tuple-element.427, f32[1024,5]{0,1:T(8,128)S(1)} %get-tuple-element.408, pred[]{:T(512)S(6)} %compare.9, bf16[5,512,64]{1,2,0:T(8,128)(2,1)S(1)} %gather_fusion.1, pred[5]{0:T(512)(128)(4,1)S(1)} %compare_and_fusion.2, f32[5,512,1024]{2,1,0:T(8,128)} %get-tuple-element.406, ...), kind=kOutput, calls=%fused_computation.15.clone.1 | convolution fusion | flops 349798400 | bytes 14000134 | tf_op jit(solution)/shard_map/while/body/eval_jaxpr/qhk,khd->qhd/dot_general | solution.py:73
  279.1 6.5 %convert_reduce_fusion.2 = f32[1024,5]{0,1:T(8,128)S(1)} fusion(f32[1024,5]{0,1:T(8,128)S(1)} %select_maximum_fusion.2, f32[5,512,1024]{2,1,0:T(8,128)} %get-tuple-element.406, pred[1024,512]{0,1:T(8,128)(4,1)S(1)} %fusion.51), kind=kLoop, calls=%fused_computation.7.clone.1 | loop fusion | flops 18344960 | bytes 11051008 | tf_op jit(solution)/shard_map/while/body/eval_jaxpr/reduce_sum | solution.py:72
  286.4 8.3 %fusion.55 = f32[1024,5,64]{0,2,1:T(8,128)} fusion(f32[1024,5,64]{0,2,1:T(8,128)} %get-tuple-element.427, f32[1024,5]{0,1:T(8,128)S(1)} %get-tuple-element.408, pred[]{:T(512)S(6)} %compare.9, bf16[5,512,64]{1,2,0:T(8,128)(2,1)S(1)} %gather_fusion.1, pred[5]{0:T(512)(128)(4,1)S(1)} %compare_and_fusion.2, f32[5,512,1024]{2,1,0:T(8,128)} %get-tuple-element.406, ...), kind=kOutput, calls=%fused_computation.15.clone.1 | convolution fusion | flops 349798400 | bytes 14000134 | tf_op jit(solution)/shard_map/while/body/eval_jaxpr/qhk,khd->qhd/dot_general | solution.py:73
  312.2 8.3 %fusion.55 = f32[1024,5,64]{0,2,1:T(8,128)} fusion(f32[1024,5,64]{0,2,1:T(8,128)} %get-tuple-element.427, f32[1024,5]{0,1:T(8,128)S(1)} %get-tuple-element.408, pred[]{:T(512)S(6)} %compare.9, bf16[5,512,64]{1,2,0:T(8,128)(2,1)S(1)} %gather_fusion.1, pred[5]{0:T(512)(128)(4,1)S(1)} %compare_and_fusion.2, f32[5,512,1024]{2,1,0:T(8,128)} %get-tuple-element.406, ...), kind=kOutput, calls=%fused_computation.15.clone.1 | convolution fusion | flops 349798400 | bytes 14000134 | tf_op jit(solution)/shard_map/while/body/eval_jaxpr/qhk,khd->qhd/dot_general | solution.py:73
  337.9 8.3 %fusion.55 = f32[1024,5,64]{0,2,1:T(8,128)} fusion(f32[1024,5,64]{0,2,1:T(8,128)} %get-tuple-element.427, f32[1024,5]{0,1:T(8,128)S(1)} %get-tuple-element.408, pred[]{:T(512)S(6)} %compare.9, bf16[5,512,64]{1,2,0:T(8,128)(2,1)S(1)} %gather_fusion.1, pred[5]{0:T(512)(128)(4,1)S(1)} %compare_and_fusion.2, f32[5,512,1024]{2,1,0:T(8,128)} %get-tuple-element.406, ...), kind=kOutput, calls=%fused_computation.15.clone.1 | convolution fusion | flops 349798400 | bytes 14000134 | tf_op jit(solution)/shard_map/while/body/eval_jaxpr/qhk,khd->qhd/dot_general | solution.py:73
  363.7 8.3 %fusion.55 = f32[1024,5,64]{0,2,1:T(8,128)} fusion(f32[1024,5,64]{0,2,1:T(8,128)} %get-tuple-element.427, f32[1024,5]{0,1:T(8,128)S(1)} %get-tuple-element.408, pred[]{:T(512)S(6)} %compare.9, bf16[5,512,64]{1,2,0:T(8,128)(2,1)S(1)} %gather_fusion.1, pred[5]{0:T(512)(128)(4,1)S(1)} %compare_and_fusion.2, f32[5,512,1024]{2,1,0:T(8,128)} %get-tuple-element.406, ...), kind=kOutput, calls=%fused_computation.15.clone.1 | convolution fusion | flops 349798400 | bytes 14000134 | tf_op jit(solution)/shard_map/while/body/eval_jaxpr/qhk,khd->qhd/dot_general | solution.py:73
  389.4 8.3 %fusion.55 = f32[1024,5,64]{0,2,1:T(8,128)} fusion(f32[1024,5,64]{0,2,1:T(8,128)} %get-tuple-element.427, f32[1024,5]{0,1:T(8,128)S(1)} %get-tuple-element.408, pred[]{:T(512)S(6)} %compare.9, bf16[5,512,64]{1,2,0:T(8,128)(2,1)S(1)} %gather_fusion.1, pred[5]{0:T(512)(128)(4,1)S(1)} %compare_and_fusion.2, f32[5,512,1024]{2,1,0:T(8,128)} %get-tuple-element.406, ...), kind=kOutput, calls=%fused_computation.15.clone.1 | convolution fusion | flops 349798400 | bytes 14000134 | tf_op jit(solution)/shard_map/while/body/eval_jaxpr/qhk,khd->qhd/dot_general | solution.py:73
  415.2 8.3 %fusion.55 = f32[1024,5,64]{0,2,1:T(8,128)} fusion(f32[1024,5,64]{0,2,1:T(8,128)} %get-tuple-element.427, f32[1024,5]{0,1:T(8,128)S(1)} %get-tuple-element.408, pred[]{:T(512)S(6)} %compare.9, bf16[5,512,64]{1,2,0:T(8,128)(2,1)S(1)} %gather_fusion.1, pred[5]{0:T(512)(128)(4,1)S(1)} %compare_and_fusion.2, f32[5,512,1024]{2,1,0:T(8,128)} %get-tuple-element.406, ...), kind=kOutput, calls=%fused_computation.15.clone.1 | convolution fusion | flops 349798400 | bytes 14000134 | tf_op jit(solution)/shard_map/while/body/eval_jaxpr/qhk,khd->qhd/dot_general | solution.py:73
  433.6 6.5 %convert_reduce_fusion.2 = f32[1024,5]{0,1:T(8,128)S(1)} fusion(f32[1024,5]{0,1:T(8,128)S(1)} %select_maximum_fusion.2, f32[5,512,1024]{2,1,0:T(8,128)} %get-tuple-element.406, pred[1024,512]{0,1:T(8,128)(4,1)S(1)} %fusion.51), kind=kLoop, calls=%fused_computation.7.clone.1 | loop fusion | flops 18344960 | bytes 11051008 | tf_op jit(solution)/shard_map/while/body/eval_jaxpr/reduce_sum | solution.py:72
  440.9 8.3 %fusion.55 = f32[1024,5,64]{0,2,1:T(8,128)} fusion(f32[1024,5,64]{0,2,1:T(8,128)} %get-tuple-element.427, f32[1024,5]{0,1:T(8,128)S(1)} %get-tuple-element.408, pred[]{:T(512)S(6)} %compare.9, bf16[5,512,64]{1,2,0:T(8,128)(2,1)S(1)} %gather_fusion.1, pred[5]{0:T(512)(128)(4,1)S(1)} %compare_and_fusion.2, f32[5,512,1024]{2,1,0:T(8,128)} %get-tuple-element.406, ...), kind=kOutput, calls=%fused_computation.15.clone.1 | convolution fusion | flops 349798400 | bytes 14000134 | tf_op jit(solution)/shard_map/while/body/eval_jaxpr/qhk,khd->qhd/dot_general | solution.py:73
  466.7 7.4 %all-to-all-start = ((bf16[32,1,64,640]{3,2,1,0:T(8,128)(2,1)}), bf16[32,1,64,640]{3,2,1,0:T(8,128)(2,1)}, u32[]{:S(2)}, u32[]{:S(2)}) async-start(bf16[32,1,64,640]{3,2,1,0:T(8,128)(2,1)} %bitcast.13), calls=%async_computation.1 | async-start | bytes 5242880 | tf_op jit(solution)/shard_map/all_to_all | solution.py:175
  474.1 6.6 %convert_element_type.52 = f32[1024,2048]{1,0:T(8,128)} convert(bf16[1024,2048]{1,0:T(8,128)(2,1)} %param.13) | non-fusion elementwise | flops 2097152 | bytes 12582912 | tf_op jit(solution)/shard_map/convert_element_type | solution.py:100
  480.7 25.8 %all-to-all-done = bf16[32,1,64,640]{3,2,1,0:T(8,128)(2,1)} async-done(((bf16[32,1,64,640]{3,2,1,0:T(8,128)(2,1)}), bf16[32,1,64,640]{3,2,1,0:T(8,128)(2,1)}, u32[]{:S(2)}, u32[]{:S(2)}) %all-to-all-start) | async-done | bytes 2621472 | tf_op jit(solution)/shard_map/all_to_all | solution.py:175
  (310 shorter events, 252.1 us)
Async XLA Ops:
  7.2 3.4 copy-start
  7.2 3.3 copy-start.4
  7.2 499.3 %reduce-scatter.2.cloned.1.call-start = ((), (), s32[]{:S(2)}) async-start(), calls=%async_computation.2 | async-start | bytes 5242880 | tf_op jit(solution)/shard_map/reduce_scatter | solution.py:167
  7.2 4.2 copy-start.2
  14.7 1.5 copy-start.3
  16.3 6.2 %slice-start = ((f32[1024,640]{0,1:T(8,128)}), f32[1024,320]{0,1:T(8,128)S(1)}, s32[]{:S(2)}) async-start(f32[1024,640]{0,1:T(8,128)} %copy-done.3), calls=%async_computation.3 | async-start | bytes 2621440 | tf_op jit(solution)/shard_map/slice | solution.py:37
  456.5 0.7 copy-start.5
  466.7 39.7 %all-to-all-start = ((bf16[32,1,64,640]{3,2,1,0:T(8,128)(2,1)}), bf16[32,1,64,640]{3,2,1,0:T(8,128)(2,1)}, u32[]{:S(2)}, u32[]{:S(2)}) async-start(bf16[32,1,64,640]{3,2,1,0:T(8,128)(2,1)} %bitcast.13), calls=%async_computation.1 | async-start | bytes 5242880 | tf_op jit(solution)/shard_map/all_to_all | solution.py:175
  506.5 6.8 %copy-start.1 = (bf16[2048,640]{1,0:T(8,128)(2,1)S(1)}, bf16[2048,640]{1,0:T(8,128)(2,1)}, u32[]{:S(2)}) copy-start(bf16[2048,640]{1,0:T(8,128)(2,1)} %param.16) | copy-start | bytes 7864324
Sparse Core Ops, SparseCore 0:
  456.6 49.1 reduce-scatter.1
where the time goes:
time: 525 us; the launch traced here: 520 us
  matrix products  239 us (46%)
  other arithmetic  170 us (32%)
  local copies, waits for them, and re-layouts  60.8 us (12%)
  waiting for transfers between devices  25.8 us (5%)
  between operations  15.6 us (3%)
  starting transfers between devices  7.4 us (1%)
    dot_general x16, matrix products, flash_local(): jnp.einsum('qhk,khd->qhd', chances, value_tile, preferred_element_type=jn...  133 us
    reduce_sum x16, other arithmetic, flash_local(): jnp.sum(chances.astype(jnp.float32), axis=-1)  104 us
    dot_general x16, matrix products, flash_local(): jnp.einsum('qhd,khd->qhk', query_heads, key_tile, preferred_element_type=...  93.3 us
    all_to_all x1, waiting for transfers between devices, shards(): lax.all_to_all(shipment, 'req', split_axis=0, concat_axis=0, tiled=True)  25.8 us
    slice x16, local copies, waits for them, and re-layouts, flash_local(): block_current[:, key_span_width:]  21.7 us
    lt x16, other arithmetic, flash_local(): columns[None, :] < cached  20.8 us
    or x16, other arithmetic, flash_local(): (columns[None, :] < cached) | (later >= 0) & (later <= row_ids[:, None])...  12.2 us
  transfers between devices with their start and end apart: 2, of which 1 were waited for; matrix products, arithmetic and copies ran while one was open for 3% of the time, Pallas kernels for 0%

commit v1 on v0

v1 whole, which is shorter than its diff:
```python
import functools

import jax
import jax.numpy as jnp
from jax import lax
from jax.experimental import pallas as pl
from jax.experimental.pallas import tpu as pltpu
from jax.sharding import PartitionSpec as P

QUERY_HEAD_COUNT = 20
KEY_VALUE_HEADS = 5
HEAD_SIZE = 64
GROUP = QUERY_HEAD_COUNT // KEY_VALUE_HEADS
NEW_TOKEN_SLOTS = 1024
PRIOR_SLOTS = 7168
SPAN = KEY_VALUE_HEADS * HEAD_SIZE
WIDTH = 2 * SPAN
LANES = 128
WINDOW = 256
LOCAL = 5
QUERY_ROWS = 256
QUERY_BLOCKS = NEW_TOKEN_SLOTS // QUERY_ROWS
STACK = LOCAL * QUERY_ROWS
KEY_ROWS = 1024
PROJECT_ROWS = 512
BLOCK_ROWS = 64
MIB = 1 << 20


def lane_ids(rows):
    return lax.broadcasted_iota(jnp.int32, (rows, LANES), 1)


def local_kv(rank, head):
    return (rank * LOCAL + head) // GROUP - rank


def key_tile_start(rank):
    return rank // 2


def value_tile_start(rank):
    return jnp.where(rank == 0, 2, 3)


def key_offset(rank):
    return rank * HEAD_SIZE - key_tile_start(rank) * LANES


def value_offset(rank):
    return SPAN + rank * HEAD_SIZE - value_tile_start(rank) * LANES


def rotate(tile, cosine, sine):
    low = lane_ids(tile.shape[0]) % HEAD_SIZE < HEAD_SIZE // 2
    half = HEAD_SIZE // 2
    other = jnp.where(low, pltpu.roll(tile, LANES - half, 1), pltpu.roll(tile, half, 1))
    return tile * cosine + other * sine


def project_kernel(
    scalars, hidden, gain, w_query, w_keyval, cosine, sine, queries, keyval, mixed_q, mixed_kv
):
    rank = scalars[2]
    fresh = scalars[1]

    @pl.when(pl.program_id(0) * PROJECT_ROWS < fresh)
    def _():
        value = hidden[...].astype(jnp.float32)
        scale = lax.rsqrt(jnp.mean(value * value, axis=-1, keepdims=True) + 1e-05)
        normed = (value * scale * gain[...].astype(jnp.float32)).astype(jnp.bfloat16)
        mixed_kv[...] = jnp.dot(normed, w_keyval[...], preferred_element_type=jnp.float32)
        mixed_q[:, :SPAN] = jnp.dot(normed, w_query[...], preferred_element_type=jnp.float32)
        cos, sin = cosine[...], sine[...]
        lanes = lane_ids(PROJECT_ROWS)
        for tile in range(WIDTH // LANES):
            columns = slice(tile * LANES, (tile + 1) * LANES)
            raw = mixed_kv[:, columns]
            if tile < 2:
                raw = rotate(raw, cos, sin)
            elif tile == 2:
                raw = jnp.where(lanes < HEAD_SIZE, rotate(raw, cos, sin), raw)
            keyval[:, columns] = raw.astype(jnp.bfloat16)
        turned = [
            rotate(mixed_q[:, tile * LANES : (tile + 1) * LANES], cos, sin) * HEAD_SIZE**-0.5
            for tile in range(3)
        ]
        swapped = [pltpu.roll(tile, HEAD_SIZE, 1) for tile in turned]
        for head in range(LOCAL):
            offset = key_offset(rank) + local_kv(rank, head) * HEAD_SIZE
            parity = (offset // HEAD_SIZE) % 2
            source = jnp.where(parity == head % 2, turned[head // 2], swapped[head // 2])
            source = jnp.where(lanes // HEAD_SIZE == parity, source, 0.0)
            for tile in range(2):
                placed = jnp.where(offset // LANES == tile, source, 0.0).astype(jnp.bfloat16)
                for part in range(PROJECT_ROWS // QUERY_ROWS):
                    queries[
                        part,
                        head * QUERY_ROWS : (head + 1) * QUERY_ROWS,
                        tile * LANES : (tile + 1) * LANES,
                    ] = placed[part * QUERY_ROWS : (part + 1) * QUERY_ROWS]

    @pl.when(pl.program_id(0) * PROJECT_ROWS >= fresh)
    def _():
        keyval[...] = jnp.zeros_like(keyval)
        queries[...] = jnp.zeros_like(queries)


def project(scalars, hidden_in, norm_gain, w_query, w_keyval, cosine, sine):
    rows, model = hidden_in.shape
    steps = rows // PROJECT_ROWS
    parts = PROJECT_ROWS // QUERY_ROWS
    return pl.pallas_call(
        project_kernel,
        out_shape=(
            jax.ShapeDtypeStruct((QUERY_BLOCKS, STACK, WINDOW), jnp.bfloat16),
            jax.ShapeDtypeStruct((rows, WIDTH), jnp.bfloat16),
        ),
        grid_spec=pltpu.PrefetchScalarGridSpec(
            num_scalar_prefetch=1,
            grid=(steps,),
            in_specs=[
                pl.BlockSpec((PROJECT_ROWS, model), lambda i, s: (i, 0)),
                pl.BlockSpec((1, model), lambda i, s: (0, 0)),
                pl.BlockSpec(w_query.shape, lambda i, s: (0, 0)),
                pl.BlockSpec(w_keyval.shape, lambda i, s: (0, 0)),
                pl.BlockSpec((PROJECT_ROWS, LANES), lambda i, s: (i, 0)),
                pl.BlockSpec((PROJECT_ROWS, LANES), lambda i, s: (i, 0)),
            ],
            out_specs=[
                pl.BlockSpec((parts, STACK, WINDOW), lambda i, s: (i, 0, 0)),
                pl.BlockSpec((PROJECT_ROWS, WIDTH), lambda i, s: (i, 0)),
            ],
            scratch_shapes=[
                pltpu.VMEM((PROJECT_ROWS, 3 * LANES), jnp.float32),
                pltpu.VMEM((PROJECT_ROWS, WIDTH), jnp.float32),
            ],
        ),
        compiler_params=pltpu.CompilerParams(vmem_limit_bytes=48 * MIB),
        cost_estimate=pl.CostEstimate(
            flops=2 * rows * model * 960, bytes_accessed=12 * MIB, transcendentals=0
        ),
        name="project",
    )(scalars, hidden_in, norm_gain.reshape(1, -1), w_query, w_keyval, cosine, sine)


def pick_kernel(scalars, picks, prior, keyval, outgoing, semaphores):
    cached, fresh = scalars[0], scalars[1]
    count = outgoing.shape[0]
    prior_blocks = PRIOR_SLOTS // BLOCK_ROWS

    def live_rows(block):
        return jnp.where(
            block < prior_blocks,
            cached - block * BLOCK_ROWS,
            fresh - (block - prior_blocks) * BLOCK_ROWS,
        )

    for slot in range(count):
        block = picks[slot]

        @pl.when((block < prior_blocks) & (live_rows(block) > 0))
        def _():
            start = pl.multiple_of(block * BLOCK_ROWS, BLOCK_ROWS)
            pltpu.make_async_copy(
                prior.at[pl.ds(start, BLOCK_ROWS)], outgoing.at[slot], semaphores.at[slot]
            ).start()

        @pl.when((block >= prior_blocks) & (live_rows(block) > 0))
        def _():
            start = pl.multiple_of((block - prior_blocks) * BLOCK_ROWS, BLOCK_ROWS)
            pltpu.make_async_copy(
                keyval.at[pl.ds(start, BLOCK_ROWS)], outgoing.at[slot], semaphores.at[slot]
            ).start()

    for slot in range(count):
        live = live_rows(picks[slot])

        @pl.when(live <= 0)
        def _():
            outgoing[slot] = jnp.zeros((BLOCK_ROWS, WIDTH), jnp.bfloat16)

        @pl.when(live > 0)
        def _():
            pltpu.make_async_copy(
                prior.at[pl.ds(0, BLOCK_ROWS)], outgoing.at[slot], semaphores.at[slot]
            ).wait()

        @pl.when((live > 0) & (live < BLOCK_ROWS))
        def _():
            rows = lax.broadcasted_iota(jnp.int32, (BLOCK_ROWS, WIDTH), 0)
            value = outgoing[slot].astype(jnp.float32)
            outgoing[slot] = jnp.where(rows < live, value, 0.0).astype(jnp.bfloat16)


def pick_blocks(scalars, picks, prior, keyval):
    count = picks.shape[0]
    return pl.pallas_call(
        pick_kernel,
        out_shape=jax.ShapeDtypeStruct((count, BLOCK_ROWS, WIDTH), jnp.bfloat16),
        grid_spec=pltpu.PrefetchScalarGridSpec(
            num_scalar_prefetch=2,
            grid=(1,),
            in_specs=[pl.BlockSpec(memory_space=pl.ANY), pl.BlockSpec(memory_space=pl.ANY)],
            out_specs=pl.BlockSpec((count, BLOCK_ROWS, WIDTH), lambda i, s, p: (0, 0, 0)),
            scratch_shapes=[pltpu.SemaphoreType.DMA((count,))],
        ),
        compiler_params=pltpu.CompilerParams(vmem_limit_bytes=16 * MIB),
        cost_estimate=pl.CostEstimate(flops=0, bytes_accessed=5 * MIB, transcendentals=0),
        name="pick_blocks",
    )(scalars, picks, prior, keyval)


def attend_kernel(
    scalars, queries, prior, fresh_rows, heads_out, keys, values, top, total, semaphores
):
    cached, fresh, rank = scalars[0], scalars[1], scalars[2]
    key_start = pl.multiple_of(key_tile_start(rank) * LANES, LANES)
    value_start = pl.multiple_of(value_tile_start(rank) * LANES, LANES)
    first = value_offset(rank)
    prior_chunks = (cached + KEY_ROWS - 1) // KEY_ROWS
    blocks = (fresh + QUERY_ROWS - 1) // QUERY_ROWS
    chunk_limit = PRIOR_SLOTS // KEY_ROWS

    def copies(chunk):
        into = pl.ds(chunk * KEY_ROWS, KEY_ROWS)
        if isinstance(chunk, int) and chunk == chunk_limit:
            source, rows = fresh_rows, pl.ds(0, NEW_TOKEN_SLOTS)
        else:
            source, rows = prior, into
        return (
            pltpu.make_async_copy(
                source.at[rows, pl.ds(key_start, WINDOW)], keys.at[into], semaphores.at[0, chunk]
            ),
            pltpu.make_async_copy(
                source.at[rows, pl.ds(value_start, WINDOW)],
                values.at[into],
                semaphores.at[1, chunk],
            ),
        )

    for copy in copies(chunk_limit):
        copy.start()
    for chunk in range(chunk_limit):

        @pl.when(chunk < prior_chunks)
        def _():
            for copy in copies(chunk):
                copy.start()

    def widen(start, rows):
        lanes = lax.broadcasted_iota(jnp.int32, (rows, WINDOW), 1)
        here = pl.ds(start, rows)
        own = (lanes >= first) & (lanes < first + 2 * HEAD_SIZE)
        raw = values[here].astype(jnp.float32)
        values[here] = jnp.where(own, raw, 1.0).astype(jnp.bfloat16)

    def arrive(chunk):
        start = pl.multiple_of(chunk * KEY_ROWS, KEY_ROWS)
        for copy in copies(chunk):
            copy.wait()
        widen(start, KEY_ROWS)
        live = cached - start

        @pl.when(live < KEY_ROWS)
        def _():
            here = pl.ds(start, KEY_ROWS)
            rows = lax.broadcasted_iota(jnp.int32, (KEY_ROWS, WINDOW), 0)
            spare = keys[0:8].astype(jnp.float32)[0:1]
            raw = keys[here].astype(jnp.float32)
            keys[here] = jnp.where(rows < live, raw, spare).astype(jnp.bfloat16)
            raw = values[here].astype(jnp.float32)
            values[here] = jnp.where(rows < live, raw, 0.0).astype(jnp.bfloat16)

    def absorb(block, start, rows, masked):
        here = pl.ds(start, rows)
        for head in range(LOCAL):
            own = slice(head * QUERY_ROWS, (head + 1) * QUERY_ROWS)
            scores = lax.dot_general(
                queries[block, own, :],
                keys[here],
                (((1,), (1,)), ((), ())),
                preferred_element_type=jnp.float32,
            )
            if masked:
                row = lax.broadcasted_iota(jnp.int32, scores.shape, 0)
                column = lax.broadcasted_iota(jnp.int32, scores.shape, 1)
                scores = jnp.where(column <= row, scores, -1e30)
            before = top[own]
            after = jnp.maximum(before, jnp.max(scores, axis=-1, keepdims=True))
            rescale = jnp.exp(before - after)
            chances = jnp.exp(scores - jnp.tile(after, (1, rows // LANES)))
            chances = chances.astype(jnp.bfloat16)
            top[own] = after
            total[own] = total[own] * jnp.tile(rescale, (1, WINDOW // LANES)) + jnp.dot(
                chances, values[here], preferred_element_type=jnp.float32
            )

    def query_block(block, carry):
        top[...] = jnp.full_like(top, -1e30)
        total[...] = jnp.zeros_like(total)

        @pl.when(block == 0)
        def _():
            for copy in copies(chunk_limit):
                copy.wait()
            widen(PRIOR_SLOTS, NEW_TOKEN_SLOTS)

        def earlier(step, inner):
            start = pl.multiple_of(PRIOR_SLOTS + step * QUERY_ROWS, QUERY_ROWS)
            absorb(block, start, QUERY_ROWS, False)
            return inner

        def cache(step, inner):
            @pl.when(block == 0)
            def _():
                arrive(step)

            start = pl.multiple_of(step * KEY_ROWS, KEY_ROWS)
            absorb(block, start, KEY_ROWS, False)
            return inner

        start = pl.multiple_of(PRIOR_SLOTS + block * QUERY_ROWS, QUERY_ROWS)
        absorb(block, start, QUERY_ROWS, True)
        lax.fori_loop(0, block, earlier, 0)
        lax.fori_loop(0, prior_chunks, cache, 0)

        lanes = lane_ids(QUERY_ROWS)
        spare = jnp.where(first == 0, LANES, 0)
        spare_tile = spare // LANES
        picked = []
        for head in range(LOCAL):
            own = slice(head * QUERY_ROWS, (head + 1) * QUERY_ROWS)
            low, high = total[own, :LANES], total[own, LANES:]
            counts = jnp.where(spare_tile == 0, low, high)
            denom = jnp.sum(jnp.where(lanes == 0, counts, 0.0), axis=-1, keepdims=True)
            offset = first + local_kv(rank, head) * HEAD_SIZE
            parity = (offset // HEAD_SIZE) % 2
            chosen = jnp.where(offset // LANES == 0, low, high)
            chosen = jnp.where(parity == head % 2, chosen, pltpu.roll(chosen, HEAD_SIZE, 1))
            picked.append(chosen / denom)
        here = pl.ds(pl.multiple_of(block * QUERY_ROWS, QUERY_ROWS), QUERY_ROWS)
        for tile in range(2):
            pair = jnp.where(lanes < HEAD_SIZE, picked[2 * tile], picked[2 * tile + 1])
            heads_out[here, tile * LANES : (tile + 1) * LANES] = pair.astype(jnp.bfloat16)
        heads_out[here, 2 * LANES :] = picked[4][:, :HEAD_SIZE].astype(jnp.bfloat16)
        return carry

    lax.fori_loop(0, blocks, query_block, 0)

    def idle(block, carry):
        here = pl.ds(pl.multiple_of(block * QUERY_ROWS, QUERY_ROWS), QUERY_ROWS)
        heads_out[here] = jnp.zeros((QUERY_ROWS, LOCAL * HEAD_SIZE), jnp.bfloat16)
        return carry

    lax.fori_loop(blocks, QUERY_BLOCKS, idle, 0)


def attend(scalars, queries, prior, fresh_rows):
    chunks = PRIOR_SLOTS // KEY_ROWS + 1
    return pl.pallas_call(
        attend_kernel,
        out_shape=jax.ShapeDtypeStruct((NEW_TOKEN_SLOTS, LOCAL * HEAD_SIZE), jnp.bfloat16),
        grid_spec=pltpu.PrefetchScalarGridSpec(
            num_scalar_prefetch=1,
            grid=(1,),
            in_specs=[
                pl.BlockSpec(queries.shape, lambda i, s: (0, 0, 0)),
                pl.BlockSpec(memory_space=pl.ANY),
                pl.BlockSpec(memory_space=pl.ANY),
            ],
            out_specs=pl.BlockSpec((NEW_TOKEN_SLOTS, LOCAL * HEAD_SIZE), lambda i, s: (0, 0)),
            scratch_shapes=[
                pltpu.VMEM((PRIOR_SLOTS + NEW_TOKEN_SLOTS, WINDOW), jnp.bfloat16),
                pltpu.VMEM((PRIOR_SLOTS + NEW_TOKEN_SLOTS, WINDOW), jnp.bfloat16),
                pltpu.VMEM((STACK, LANES), jnp.float32),
                pltpu.VMEM((STACK, WINDOW), jnp.float32),
                pltpu.SemaphoreType.DMA((2, chunks)),
            ],
        ),
        compiler_params=pltpu.CompilerParams(vmem_limit_bytes=48 * MIB),
        cost_estimate=pl.CostEstimate(
            flops=4 * 5120 * 7680 * 256, bytes_accessed=12 * MIB, transcendentals=5120 * 7680
        ),
        name="attend",
    )(scalars, queries, prior, fresh_rows)


def finish_kernel(scalars, heads, w_out, hidden, result):
    rank, fresh = scalars[2], scalars[1]
    mixed = jnp.zeros(result.shape, jnp.float32)
    for part in range(heads.shape[0]):
        mixed = mixed + jnp.dot(
            heads[part], w_out[part], preferred_element_type=jnp.float32
        )
    rows = lax.broadcasted_iota(jnp.int32, result.shape, 0) + rank * result.shape[0]
    value = hidden[...].astype(jnp.float32) + mixed
    result[...] = jnp.where(rows < fresh, value, 0.0).astype(jnp.bfloat16)


def finish(scalars, heads, w_out, hidden_in):
    parts, rows, columns = heads.shape
    model = w_out.shape[1]
    tile = 512
    return pl.pallas_call(
        finish_kernel,
        out_shape=jax.ShapeDtypeStruct((rows, model), jnp.bfloat16),
        grid_spec=pltpu.PrefetchScalarGridSpec(
            num_scalar_prefetch=1,
            grid=(model // tile,),
            in_specs=[
                pl.BlockSpec(heads.shape, lambda i, s: (0, 0, 0)),
                pl.BlockSpec((parts, columns, tile), lambda i, s: (0, 0, i)),
                pl.BlockSpec((rows, tile), lambda i, s: (s[2], i)),
            ],
            out_specs=pl.BlockSpec((rows, tile), lambda i, s: (0, i)),
        ),
        compiler_params=pltpu.CompilerParams(vmem_limit_bytes=32 * MIB),
        cost_estimate=pl.CostEstimate(
            flops=2 * rows * parts * columns * model, bytes_accessed=8 * MIB, transcendentals=0
        ),
        name="finish",
    )(scalars, heads, w_out.reshape(parts, columns, model), hidden_in)


def shards(
    hidden_in,
    norm_gain,
    w_query,
    key_value_weight,
    w_out,
    prior_cache,
    cache_len,
    group_len,
    page_map,
):
    rank = lax.axis_index("tp").astype(jnp.int32)
    tp_count = lax.axis_size("tp")
    req_count = lax.axis_size("req")
    scalars = jnp.stack([cache_len[0], group_len[0], rank])

    half_size = HEAD_SIZE // 2
    frequency = 10000.0 ** (-(jnp.arange(half_size, dtype=jnp.float32) * 2.0 / HEAD_SIZE))
    positions = cache_len[0] + jnp.arange(NEW_TOKEN_SLOTS, dtype=jnp.int32)
    angles = positions.astype(jnp.float32)[:, None] * jnp.tile(frequency, 4)[None, :]
    sign = jnp.where(jnp.arange(LANES) % HEAD_SIZE < half_size, -1.0, 1.0)
    cosine = jnp.cos(angles)
    sine = jnp.sin(angles) * sign[None, :]

    targets = jnp.arange(req_count, dtype=jnp.int32) * tp_count + rank
    order = jnp.arange(page_map.shape[1], dtype=jnp.int32)
    picks = jnp.sum(
        jnp.where(page_map[0][None, :] == targets[:, None], order[None, :], 0), axis=1
    ).astype(jnp.int32)

    prior = prior_cache[0]
    queries, keyval = project(
        scalars, hidden_in, norm_gain, w_query, key_value_weight, cosine, sine
    )
    outgoing = pick_blocks(scalars, picks, prior, keyval)
    received = lax.all_to_all(outgoing, "req", split_axis=0, concat_axis=0, tiled=True)
    decode_kv = received[None]
    attended = attend(scalars, queries, prior, keyval)
    parts = attended.reshape(tp_count, NEW_TOKEN_SLOTS // tp_count, LOCAL * HEAD_SIZE)
    heads = lax.all_to_all(parts, "tp", split_axis=0, concat_axis=0, tiled=True)
    hidden_out = finish(scalars, heads, w_out, hidden_in)
    return (hidden_out, decode_kv)


def solution(mesh):
    placed = (
        P("req", None),
        P(),
        P(None, "tp"),
        P(),
        P(),
        P("req", None, None),
        P("req"),
        P("req"),
        P("req", None),
    )
    return jax.shard_map(
        shards,
        mesh=mesh,
        in_specs=placed,
        out_specs=(P(("req", "tp"), None), P(("req", "tp"), None, None, None)),
        check_vma=False,
    )
```

time: 525 us -> 156 us (0.30)
  matrix products: 239 us -> 0 us
  other arithmetic: 170 us -> 2.18 us
  starting transfers between devices: 7.4 us -> 85.4 us
  local copies, waits for them, and re-layouts: 60.8 us -> 17.6 us
  Pallas kernels: 0 us -> 21.9 us
  between operations: 15.6 us -> 2.03 us
    dot_general x35 -> x0, matrix products: 239 us -> none  [the longest x16 133 us: flash_local(): jnp.einsum('qhk,khd->qhd', chances, value_tile, preferred_element_type=jn...]
    reduce_sum x17 -> x1, other arithmetic: 107 us -> 0.18 us  [shards(): jnp.sum(jnp.where(page_map[0][None, :] == targets[:, None], order[None, :...]
    all_to_all x1 -> x2, starting transfers between devices: 7.36 us -> 85.4 us  [the longest x1 80.1 us: shards(): lax.all_to_all(outgoing, 'req', split_axis=0, concat_axis=0, tiled=True)]
    gather x34 -> x0, local copies, waits for them, and re-layouts: 25.2 us -> none  [the longest x16 9.09 us: flash_local(): jnp.take(block_current[:, key_span_width:].reshape(KEYS_PER_BLOCK, KEY_VA...]
    pallas_call x0 -> x4, Pallas kernels: none -> 21.9 us  [the longest x1 8.47 us: project(): pl.pallas_call(project_kernel, out_shape=(jax.ShapeDtypeStruct((QUERY_BLO...]
    slice x19 -> x0, local copies, waits for them, and re-layouts: 21.8 us -> none  [the longest x16 21.7 us: flash_local(): block_current[:, key_span_width:]]
    lt x18 -> x0, other arithmetic: 20.8 us -> none  [the longest x16 20.8 us: flash_local(): columns[None, :] < cached]
    or x16 -> x0, other arithmetic: 12.2 us -> none  [flash_local(): (columns[None, :] < cached) | (later >= 0) & (later <= row_ids[:, None])...]
  transfers between devices with their start and end apart: 2 -> 2, of which waited for: 1 -> 2; matrix products, arithmetic and copies ran while one was open for 3% -> 0% of each run, Pallas kernels for 0% -> 5%
where the time goes in v1:
time: 156 us; the launch traced here: 153 us
  starting transfers between devices  85.4 us (55%)
  waiting for transfers between devices  23.9 us (15%)
  Pallas kernels  21.9 us (14%)
  local copies, waits for them, and re-layouts  17.6 us (11%)
  other arithmetic  2.18 us (1%)
  between operations  2.03 us (1%)
    all_to_all x1, starting transfers between devices, shards(): lax.all_to_all(outgoing, 'req', split_axis=0, concat_axis=0, tiled=True)  80.1 us
    all_to_all x1, waiting for transfers between devices, shards(): lax.all_to_all(outgoing, 'req', split_axis=0, concat_axis=0, tiled=True)  22.7 us
    unnamed x12, local copies, waits for them, and re-layouts  15.3 us
    pallas_call x1, Pallas kernels, project(): pl.pallas_call(project_kernel, out_shape=(jax.ShapeDtypeStruct((QUERY_BLO...  8.47 us
    all_to_all x1, starting transfers between devices, shards(): heads = lax.all_to_all(parts, 'tp', split_axis=0, concat_axis=0, tiled=True)  5.3 us
    pallas_call x1, Pallas kernels, attend(): pl.pallas_call(attend_kernel, out_shape=jax.ShapeDtypeStruct((NEW_TOKEN_S...  5.01 us
    pallas_call x1, Pallas kernels, finish(): pl.pallas_call(finish_kernel, out_shape=jax.ShapeDtypeStruct((rows, model...  4.61 us
    pallas_call x1, Pallas kernels, pick_blocks(): pl.pallas_call(pick_kernel, out_shape=jax.ShapeDtypeStruct((count, BLOCK_...  3.8 us
  transfers between devices with their start and end apart: 2, of which 2 were waited for; matrix products, arithmetic and copies ran while one was open for 0% of the time, Pallas kernels for 5%

profile of v1, /device:TPU:24, one launch (start us, length us, event | category | flops | bytes accessed | tf_op | source)
XLA Modules:
  0.0 152.9 jit_solution(13361669739699877797)
XLA Ops:
  2.0 0.1 mul.37
  2.1 0.7 reshape.41.gain
  2.7 1.8 %copy.15.w_query = bf16[2048,320]{1,0:T(8,128)(2,1)S(1)} copy(bf16[2048,320]{0,1:T(8,128)(2,1)} %param.11) | data formatting | bytes 2621440 | tf_op args[2]
  4.6 0.1 pad_add_fusion.scalars
  4.7 1.9 %fusion = (f32[1024,128]{1,0:T(8,128)S(1)}, f32[1024,128]{1,0:T(8,128)S(1)}) fusion(f32[128]{0:T(128)S(1)} %compare_select_fusion, f32[128]{0:T(128)S(1)} %mul.37, f32[1024]{0:T(1024)S(1)} %add_convert_fusion), kind=kLoop, calls=%fused_computation.2 | loop fusion | flops 262144 | bytes 1053696 | tf_op jit(solution)/shard_map/mul | solution.py:448
  6.6 8.5 %project.1 = (bf16[4,1280,256]{2,1,0:T(8,128)(2,1)}, bf16[1024,640]{1,0:T(8,128)(2,1)S(1)}) custom-call(s32[3]{0:T(128)S(1)} %pad_add_fusion.scalars, bf16[1024,2048]{1,0:T(8,128)(2,1)} %hidden.3, bf16[1,2048]{1,0:T(2,128)(2,1)S(1)} %reshape.41.gain, bf16[2048,320]{1,0:T(8,128)(2,1)S(1)} %copy.15.w_query, bf16[2048,640]{1,0:T(8,128)(2,1)} %w_keyval.1, ...), custom_call_target="tpu_custom_call" | custom-call | flops 4026531840 | bytes 12582912 | tf_op jit(solution)/shard_map/project/pallas_call | solution.py:113
  15.0 0.0 copy-start.3
  15.0 1.7 %copy-done.3 = bf16[4,1280,256]{2,1,0:T(8,128)(2,1)S(1)} copy-done((bf16[4,1280,256]{2,1,0:T(8,128)(2,1)S(1)}, bf16[4,1280,256]{2,1,0:T(8,128)(2,1)}, u32[]{:S(2)}) %copy-start.3) | copy-done | bytes 2621464
  16.8 5.0 %attend.1 = bf16[1024,320]{1,0:T(8,128)(2,1)S(1)} custom-call(s32[3]{0:T(128)S(1)} %pad_add_fusion.scalars, bf16[4,1280,256]{2,1,0:T(8,128)(2,1)S(1)} %copy-done.3, bf16[7168,640]{1,0:T(8,128)(2,1)} %bitcast.8, bf16[1024,640]{1,0:T(8,128)(2,1)S(1)} %get-tuple-element.5.fresh_rows.keyval), custom_call_target="tpu_custom_call" | custom-call | flops 40265318400 | bytes 12582912 | tf_op jit(solution)/shard_map/attend/pallas_call | solution.py:361
  21.8 0.0 copy-start.4
  21.8 1.1 copy.16
  22.9 5.3 %all-to-all-start = ((bf16[4,256,320]{1,2,0:T(8,128)(2,1)}), bf16[4,256,320]{1,2,0:T(8,128)(2,1)S(1)}, u32[]{:S(2)}, u32[]{:S(2)}) async-start(bf16[4,256,320]{1,2,0:T(8,128)(2,1)} %copy.16), calls=%async_computation | async-start | bytes 1310720 | tf_op jit(solution)/shard_map/all_to_all | solution.py:465
  28.2 0.0 copy-done.4
  28.2 0.2 select_reduce_fusion.picks
  28.4 0.0 copy-start
  28.4 3.6 %copy-done = bf16[1,7168,640]{2,1,0:T(8,128)(2,1)S(1)} copy-done((bf16[1,7168,640]{2,1,0:T(8,128)(2,1)S(1)}, bf16[1,7168,640]{2,1,0:T(8,128)(2,1)}, u32[]{:S(2)}) %copy-start) | copy-done | bytes 9175064
  32.0 3.8 %pick_blocks.1 = bf16[32,64,640]{2,1,0:T(8,128)(2,1)} custom-call(s32[3]{0:T(128)S(1)} %pad_add_fusion.scalars, s32[32]{0:T(128)S(1)} %select_reduce_fusion.picks, bf16[7168,640]{1,0:T(8,128)(2,1)S(1)} %bitcast.9, bf16[1024,640]{1,0:T(8,128)(2,1)S(1)} %get-tuple-element.5.fresh_rows.keyval), custom_call_target="tpu_custom_call" | custom-call | bytes 5242880 | tf_op jit(solution)/shard_map/pick_blocks/pallas_call | solution.py:198
  35.8 1.2 all-to-all-done
  37.0 80.1 %all-to-all-start.1 = ((bf16[32,64,640]{2,1,0:T(8,128)(2,1)}), bf16[32,64,640]{2,1,0:T(8,128)(2,1)}, u32[]{:S(2)}, u32[]{:S(2)}) async-start(bf16[32,64,640]{2,1,0:T(8,128)(2,1)} %pick_blocks.1), calls=%async_computation.1 | async-start | bytes 5242880 | tf_op jit(solution)/shard_map/all_to_all | solution.py:461
  117.1 0.4 copy.17.heads
  117.5 0.0 copy-start.1
  117.5 2.5 %copy-done.1 = bf16[1280,2048]{1,0:T(8,128)(2,1)S(1)} copy-done((bf16[1280,2048]{1,0:T(8,128)(2,1)S(1)}, bf16[1280,2048]{1,0:T(8,128)(2,1)}, u32[]{:S(2)}) %copy-start.1) | copy-done | bytes 5242904
  120.0 0.0 copy-start.2
  120.0 2.2 %copy-done.2 = bf16[1024,2048]{1,0:T(8,128)(2,1)S(1)} copy-done((bf16[1024,2048]{1,0:T(8,128)(2,1)S(1)}, bf16[1024,2048]{1,0:T(8,128)(2,1)}, u32[]{:S(2)}) %copy-start.2) | copy-done | bytes 4194328
  122.2 4.6 %finish.1 = bf16[256,2048]{1,0:T(8,128)(2,1)} custom-call(s32[3]{0:T(128)S(1)} %pad_add_fusion.scalars, bf16[4,256,320]{2,1,0:T(8,128)(2,1)S(1)} %copy.17.heads, bf16[4,320,2048]{2,1,0:T(8,128)(2,1)S(1)} %bitcast.10, bf16[1024,2048]{1,0:T(8,128)(2,1)S(1)} %copy-done.2), custom_call_target="tpu_custom_call" | custom-call | flops 1342177280 | bytes 8388608 | tf_op jit(solution)/shard_map/finish/pallas_call | solution.py:405
  126.8 22.7 %all-to-all-done.1 = bf16[32,64,640]{2,1,0:T(8,128)(2,1)} async-done(((bf16[32,64,640]{2,1,0:T(8,128)(2,1)}), bf16[32,64,640]{2,1,0:T(8,128)(2,1)}, u32[]{:S(2)}, u32[]{:S(2)}) %all-to-all-start.1) | async-done | bytes 2621472 | tf_op jit(solution)/shard_map/all_to_all | solution.py:461
  149.5 3.5 %copy.21 = bf16[1,32,64,640]{3,2,1,0:T(8,128)(2,1)} copy(bf16[1,32,64,640]{3,2,1,0:T(8,128)(2,1)} %bitcast.6) | data formatting | bytes 5242880
  (5 shorter events, 0.0 us)
Async XLA Ops:
  15.0 1.7 %copy-start.3 = (bf16[4,1280,256]{2,1,0:T(8,128)(2,1)S(1)}, bf16[4,1280,256]{2,1,0:T(8,128)(2,1)}, u32[]{:S(2)}) copy-start(bf16[4,1280,256]{2,1,0:T(8,128)(2,1)} %get-tuple-element.4.queries) | copy-start | bytes 7864324
  21.8 6.4 %copy-start.4 = (s32[1,128]{1,0:T(1,128)S(1)}, s32[1,128]{1,0:T(1,128)}, u32[]{:S(2)}) copy-start(s32[1,128]{1,0:T(1,128)} %param.17) | copy-start | bytes 1540
  22.9 14.1 %all-to-all-start = ((bf16[4,256,320]{1,2,0:T(8,128)(2,1)}), bf16[4,256,320]{1,2,0:T(8,128)(2,1)S(1)}, u32[]{:S(2)}, u32[]{:S(2)}) async-start(bf16[4,256,320]{1,2,0:T(8,128)(2,1)} %copy.16), calls=%async_computation | async-start | bytes 1310720 | tf_op jit(solution)/shard_map/all_to_all | solution.py:465
  28.4 3.6 %copy-start = (bf16[1,7168,640]{2,1,0:T(8,128)(2,1)S(1)}, bf16[1,7168,640]{2,1,0:T(8,128)(2,1)}, u32[]{:S(2)}) copy-start(bf16[1,7168,640]{2,1,0:T(8,128)(2,1)} %param.14) | copy-start | bytes 27525124
  37.0 112.5 %all-to-all-start.1 = ((bf16[32,64,640]{2,1,0:T(8,128)(2,1)}), bf16[32,64,640]{2,1,0:T(8,128)(2,1)}, u32[]{:S(2)}, u32[]{:S(2)}) async-start(bf16[32,64,640]{2,1,0:T(8,128)(2,1)} %pick_blocks.1), calls=%async_computation.1 | async-start | bytes 5242880 | tf_op jit(solution)/shard_map/all_to_all | solution.py:461
  117.5 2.5 %copy-start.1 = (bf16[1280,2048]{1,0:T(8,128)(2,1)S(1)}, bf16[1280,2048]{1,0:T(8,128)(2,1)}, u32[]{:S(2)}) copy-start(bf16[1280,2048]{1,0:T(8,128)(2,1)} %param.13) | copy-start | bytes 15728644
  120.0 2.2 %copy-start.2 = (bf16[1024,2048]{1,0:T(8,128)(2,1)S(1)}, bf16[1024,2048]{1,0:T(8,128)(2,1)}, u32[]{:S(2)}) copy-start(bf16[1024,2048]{1,0:T(8,128)(2,1)} %hidden.3) | copy-start | bytes 12582916

commit v2 on v1

v2 whole, which is shorter than its diff:
```python
import jax
import jax.numpy as jnp
from jax import lax
from jax.experimental import pallas as pl
from jax.experimental.pallas import tpu as pltpu
from jax.sharding import PartitionSpec as P

QUERY_HEAD_COUNT = 20
KEY_VALUE_HEADS = 5
HEAD_SIZE = 64
GROUP = QUERY_HEAD_COUNT // KEY_VALUE_HEADS
NEW_TOKEN_SLOTS = 1024
PRIOR_SLOTS = 7168
SPAN = KEY_VALUE_HEADS * HEAD_SIZE
WIDTH = 2 * SPAN
LANES = 128
WINDOW = 256
LOCAL = 5
QUERY_ROWS = 512
QUERY_BLOCKS = NEW_TOKEN_SLOTS // QUERY_ROWS
STACK = LOCAL * QUERY_ROWS
KEY_ROWS = 1024
PREPARE_ROWS = 256
PROJECT_ROWS = 512
NORM_ROWS = 256
PART_ROWS = 256
FINISH_COLUMNS = 512
PACKED = PART_ROWS * LOCAL // 2
BLOCK_ROWS = 64
MIB = 1 << 20


def lane_ids(rows):
    return lax.broadcasted_iota(jnp.int32, (rows, LANES), 1)


def local_kv(rank, head):
    return (rank * LOCAL + head) // GROUP - rank


def key_tile_start(rank):
    return rank // 2


def value_tile_start(rank):
    return jnp.where(rank == 0, 2, 3)


def key_offset(rank):
    return rank * HEAD_SIZE - key_tile_start(rank) * LANES


def value_offset(rank):
    return SPAN + rank * HEAD_SIZE - value_tile_start(rank) * LANES


def rotate(tile, cosine, sine):
    low = lane_ids(tile.shape[0]) % HEAD_SIZE < HEAD_SIZE // 2
    half = HEAD_SIZE // 2
    other = jnp.where(low, pltpu.roll(tile, LANES - half, 1), pltpu.roll(tile, half, 1))
    return tile * cosine + other * sine


def project_kernel(
    hidden_hbm,
    gain,
    w_query_hbm,
    w_keyval_hbm,
    cosine,
    sine,
    queries,
    keyval,
    hidden,
    w_query,
    w_keyval,
    normed,
    mixed_q,
    mixed_kv,
    semaphores,
):
    total = hidden.shape[0]
    pieces = total // NORM_ROWS
    loads = [
        pltpu.make_async_copy(
            hidden_hbm.at[pl.ds(piece * NORM_ROWS, NORM_ROWS)],
            hidden.at[pl.ds(piece * NORM_ROWS, NORM_ROWS)],
            semaphores.at[piece],
        )
        for piece in range(pieces)
    ]
    weights = [
        pltpu.make_async_copy(w_keyval_hbm, w_keyval, semaphores.at[pieces]),
        pltpu.make_async_copy(w_query_hbm, w_query, semaphores.at[pieces + 1]),
    ]
    for copy in loads[:2] + weights + loads[2:]:
        copy.start()

    def norm(piece):
        here = pl.ds(piece * NORM_ROWS, NORM_ROWS)
        value = hidden[here].astype(jnp.float32)
        scale = lax.rsqrt(jnp.mean(value * value, axis=-1, keepdims=True) + 1e-05)
        normed[here] = (value * scale * gain[...].astype(jnp.float32)).astype(jnp.bfloat16)

    lanes = lane_ids(PROJECT_ROWS)

    def mix(block):
        here = pl.ds(block * PROJECT_ROWS, PROJECT_ROWS)
        rows = normed[here]
        mixed_kv[here] = jnp.dot(rows, w_keyval[...], preferred_element_type=jnp.float32)
        mixed_q[here, :SPAN] = lax.dot_general(
            rows, w_query[...], (((1,), (1,)), ((), ())), preferred_element_type=jnp.float32
        )

    def turn(block):
        here = pl.ds(block * PROJECT_ROWS, PROJECT_ROWS)
        cos, sin = cosine[here], sine[here]
        for tile in range(WIDTH // LANES):
            columns = slice(tile * LANES, (tile + 1) * LANES)
            raw = mixed_kv[here, columns]
            if tile < 2:
                raw = rotate(raw, cos, sin)
            elif tile == 2:
                raw = jnp.where(lanes < HEAD_SIZE, rotate(raw, cos, sin), raw)
            keyval[here, columns] = raw.astype(jnp.bfloat16)
        for head in range(LOCAL):
            tile = head // 2
            raw = mixed_q[here, tile * LANES : (tile + 1) * LANES]
            turned = rotate(raw, cos, sin) * HEAD_SIZE**-0.5
            if head % 2:
                turned = pltpu.roll(turned, HEAD_SIZE, 1)
            queries[block, head * QUERY_ROWS : (head + 1) * QUERY_ROWS] = turned[
                :, :HEAD_SIZE
            ].astype(jnp.bfloat16)

    for piece in range(2):
        loads[piece].wait()
        norm(piece)
    for copy in weights + loads[2:]:
        copy.wait()
    mix(0)
    norm(2)
    norm(3)
    mix(1)
    turn(0)
    turn(1)


def project(hidden_in, norm_gain, w_query, w_keyval, cosine, sine):
    rows, model = hidden_in.shape
    vector = pl.BlockSpec(memory_space=pltpu.VMEM)
    far = pl.BlockSpec(memory_space=pltpu.HBM)
    return pl.pallas_call(
        project_kernel,
        out_shape=(
            jax.ShapeDtypeStruct((QUERY_BLOCKS, STACK, HEAD_SIZE), jnp.bfloat16),
            jax.ShapeDtypeStruct((rows, WIDTH), jnp.bfloat16),
        ),
        in_specs=[far, vector, far, far, vector, vector],
        out_specs=[vector, vector],
        scratch_shapes=[
            pltpu.VMEM((rows, model), jnp.bfloat16),
            pltpu.VMEM((SPAN, model), jnp.bfloat16),
            pltpu.VMEM((model, WIDTH), jnp.bfloat16),
            pltpu.VMEM((rows, model), jnp.bfloat16),
            pltpu.VMEM((rows, 3 * LANES), jnp.float32),
            pltpu.VMEM((rows, WIDTH), jnp.float32),
            pltpu.SemaphoreType.DMA((rows // NORM_ROWS + 2,)),
        ],
        compiler_params=pltpu.CompilerParams(vmem_limit_bytes=58 * MIB),
        cost_estimate=pl.CostEstimate(
            flops=2 * rows * model * (SPAN + WIDTH), bytes_accessed=10 * MIB, transcendentals=0
        ),
        name="project",
    )(hidden_in, norm_gain.reshape(1, -1), w_query.T, w_keyval, cosine, sine)


def pick_kernel(scalars, picks, prior, keyval, outgoing, semaphores):
    cached, fresh = scalars[0], scalars[1]
    count = outgoing.shape[0]
    prior_blocks = PRIOR_SLOTS // BLOCK_ROWS

    def live_rows(block):
        return jnp.where(
            block < prior_blocks,
            cached - block * BLOCK_ROWS,
            fresh - (block - prior_blocks) * BLOCK_ROWS,
        )

    for slot in range(count):
        block = picks[slot]

        @pl.when((block < prior_blocks) & (live_rows(block) > 0))
        def _():
            start = pl.multiple_of(block * BLOCK_ROWS, BLOCK_ROWS)
            pltpu.make_async_copy(
                prior.at[pl.ds(start, BLOCK_ROWS)], outgoing.at[slot], semaphores.at[slot]
            ).start()

        @pl.when((block >= prior_blocks) & (live_rows(block) > 0))
        def _():
            start = pl.multiple_of((block - prior_blocks) * BLOCK_ROWS, BLOCK_ROWS)
            pltpu.make_async_copy(
                keyval.at[pl.ds(start, BLOCK_ROWS)], outgoing.at[slot], semaphores.at[slot]
            ).start()

    for slot in range(count):
        live = live_rows(picks[slot])

        @pl.when(live <= 0)
        def _():
            outgoing[slot] = jnp.zeros((BLOCK_ROWS, WIDTH), jnp.bfloat16)

        @pl.when(live > 0)
        def _():
            pltpu.make_async_copy(
                prior.at[pl.ds(0, BLOCK_ROWS)], outgoing.at[slot], semaphores.at[slot]
            ).wait()

        @pl.when((live > 0) & (live < BLOCK_ROWS))
        def _():
            rows = lax.broadcasted_iota(jnp.int32, (BLOCK_ROWS, WIDTH), 0)
            value = outgoing[slot].astype(jnp.float32)
            outgoing[slot] = jnp.where(rows < live, value, 0.0).astype(jnp.bfloat16)


def pick_blocks(scalars, picks, prior, keyval):
    count = picks.shape[0]
    return pl.pallas_call(
        pick_kernel,
        out_shape=jax.ShapeDtypeStruct((count, BLOCK_ROWS, WIDTH), jnp.bfloat16),
        grid_spec=pltpu.PrefetchScalarGridSpec(
            num_scalar_prefetch=2,
            grid=(1,),
            in_specs=[
                pl.BlockSpec(memory_space=pltpu.HBM),
                pl.BlockSpec(memory_space=pl.ANY),
            ],
            out_specs=pl.BlockSpec((count, BLOCK_ROWS, WIDTH), lambda i, s, p: (0, 0, 0)),
            scratch_shapes=[pltpu.SemaphoreType.DMA((count,))],
        ),
        compiler_params=pltpu.CompilerParams(vmem_limit_bytes=56 * MIB),
        cost_estimate=pl.CostEstimate(flops=0, bytes_accessed=5 * MIB, transcendentals=0),
        name="pick_blocks",
    )(scalars, picks, prior, keyval)


def attend_kernel(
    scalars,
    queries,
    prior,
    fresh_rows,
    heads_out,
    raw_keys,
    raw_values,
    keys,
    values,
    top,
    total,
    semaphores,
):
    cached, fresh, rank = scalars[0], scalars[1], scalars[2]
    key_start = pl.multiple_of(key_tile_start(rank) * LANES, LANES)
    value_start = pl.multiple_of(value_tile_start(rank) * LANES, LANES)
    key_shift, value_shift = key_offset(rank), value_offset(rank)
    prior_chunks = (cached + KEY_ROWS - 1) // KEY_ROWS
    blocks = (fresh + QUERY_ROWS - 1) // QUERY_ROWS
    chunk_limit = PRIOR_SLOTS // KEY_ROWS

    def copies(chunk):
        into = pl.ds(chunk * KEY_ROWS, KEY_ROWS)
        return (
            pltpu.make_async_copy(
                prior.at[into, pl.ds(key_start, WINDOW)],
                raw_keys.at[into],
                semaphores.at[0, chunk],
            ),
            pltpu.make_async_copy(
                prior.at[into, pl.ds(value_start, WINDOW)],
                raw_values.at[into],
                semaphores.at[1, chunk],
            ),
        )

    into = pl.ds(PRIOR_SLOTS, NEW_TOKEN_SLOTS)
    fresh_copies = (
        pltpu.make_async_copy(
            fresh_rows.at[:, pl.ds(key_start, WINDOW)],
            raw_keys.at[into],
            semaphores.at[0, chunk_limit],
        ),
        pltpu.make_async_copy(
            fresh_rows.at[:, pl.ds(value_start, WINDOW)],
            raw_values.at[into],
            semaphores.at[1, chunk_limit],
        ),
    )
    for copy in fresh_copies:
        copy.start()
    for chunk in range(chunk_limit):

        @pl.when(chunk < prior_chunks)
        def _():
            for copy in copies(chunk):
                copy.start()

    def prepare(start, live):
        here = pl.ds(start, PREPARE_ROWS)
        lanes = lane_ids(PREPARE_ROWS)
        alive = lax.broadcasted_iota(jnp.int32, (PREPARE_ROWS, LANES), 0) < live
        raw = raw_keys[here].astype(jnp.float32)
        low, high = raw[:, :LANES], raw[:, LANES:]
        spare = raw_keys[0:8].astype(jnp.float32)[0:1]
        low = jnp.where(alive, low, spare[:, :LANES])
        high = jnp.where(alive, high, spare[:, LANES:])
        joined = jnp.where(
            lanes < HEAD_SIZE, pltpu.roll(low, HEAD_SIZE, 1), pltpu.roll(high, HEAD_SIZE, 1)
        )
        pair = jnp.where(key_shift == 0, low, joined)
        keys[:, here] = pair.T.astype(jnp.bfloat16)
        raw = raw_values[here].astype(jnp.float32)
        low, high = raw[:, :LANES], raw[:, LANES:]
        low_turned, high_turned = pltpu.roll(low, HEAD_SIZE, 1), pltpu.roll(high, HEAD_SIZE, 1)
        one = jnp.where(
            value_shift == 0, low, jnp.where(value_shift == HEAD_SIZE, low_turned, high)
        )
        two = jnp.where(
            value_shift == 0, low_turned, jnp.where(value_shift == HEAD_SIZE, high, high_turned)
        )
        for slot, own in enumerate((one, two)):
            own = jnp.where(alive, jnp.where(lanes < HEAD_SIZE, own, 1.0), 0.0)
            values[slot, here] = own.astype(jnp.bfloat16)

    def score(block, head, start, rows):
        which = local_kv(rank, head)
        return jnp.dot(
            queries[block, head * QUERY_ROWS : (head + 1) * QUERY_ROWS],
            keys[pl.ds(pl.multiple_of(which * HEAD_SIZE, HEAD_SIZE), HEAD_SIZE), pl.ds(start, rows)],
            preferred_element_type=jnp.float32,
        )

    def blend(head, start, rows, scores, masked):
        own = slice(head * QUERY_ROWS, (head + 1) * QUERY_ROWS)
        if masked:
            row = lax.broadcasted_iota(jnp.int32, scores.shape, 0)
            column = lax.broadcasted_iota(jnp.int32, scores.shape, 1)
            scores = jnp.where(column <= row, scores, -1e30)
        before = top[own]
        after = jnp.maximum(before, jnp.max(scores, axis=-1, keepdims=True))
        rescale = jnp.exp(before - after)
        chances = jnp.exp(scores - jnp.tile(after, (1, rows // LANES))).astype(jnp.bfloat16)
        top[own] = after
        total[own] = total[own] * rescale + jnp.dot(
            chances,
            values[local_kv(rank, head), pl.ds(start, rows)],
            preferred_element_type=jnp.float32,
        )

    def absorb(block, start, rows, masked):
        pending = score(block, 0, start, rows)
        for head in range(LOCAL):
            following = score(block, head + 1, start, rows) if head + 1 < LOCAL else None
            blend(head, start, rows, pending, masked)
            pending = following

    def query_block(block, carry):
        top[...] = jnp.full_like(top, -1e30)
        total[...] = jnp.zeros_like(total)

        @pl.when(block == 0)
        def _():
            for copy in fresh_copies:
                copy.wait()

            def each(step, inner):
                start = pl.multiple_of(PRIOR_SLOTS + step * PREPARE_ROWS, PREPARE_ROWS)
                prepare(start, PREPARE_ROWS)
                return inner

            lax.fori_loop(0, NEW_TOKEN_SLOTS // PREPARE_ROWS, each, 0)

        def earlier(step, inner):
            start = pl.multiple_of(PRIOR_SLOTS + step * QUERY_ROWS, QUERY_ROWS)
            absorb(block, start, QUERY_ROWS, False)
            return inner

        def cache(step, inner):
            start = pl.multiple_of(step * KEY_ROWS, KEY_ROWS)

            @pl.when(block == 0)
            def _():
                for copy in copies(step):
                    copy.wait()

                def each(part, most):
                    here = pl.multiple_of(start + part * PREPARE_ROWS, PREPARE_ROWS)
                    prepare(here, cached - here)
                    return most

                lax.fori_loop(0, KEY_ROWS // PREPARE_ROWS, each, 0)

            absorb(block, start, KEY_ROWS, False)
            return inner

        start = pl.multiple_of(PRIOR_SLOTS + block * QUERY_ROWS, QUERY_ROWS)
        absorb(block, start, QUERY_ROWS, True)
        lax.fori_loop(0, block, earlier, 0)
        lax.fori_loop(0, prior_chunks, cache, 0)

        lanes = lane_ids(QUERY_ROWS)
        odd = rank % 2 == 1
        plain, turned = [], []
        for head in range(LOCAL):
            sums = total[head * QUERY_ROWS : (head + 1) * QUERY_ROWS]
            swapped = pltpu.roll(sums, HEAD_SIZE, 1)
            plain.append(sums / swapped)
            turned.append(swapped / sums)
        even_pairs = [jnp.where(lanes < HEAD_SIZE, plain[i], turned[i + 1]) for i in (0, 2)]
        odd_pairs = [jnp.where(lanes < HEAD_SIZE, plain[i], turned[i + 1]) for i in (1, 3)]
        single = jnp.where(odd, plain[0], plain[4])
        single_turned = jnp.where(odd, turned[0], turned[4])
        near = (lane_ids(LANES) < HEAD_SIZE) != odd
        for part in range(QUERY_ROWS // PART_ROWS):
            slot = block * (QUERY_ROWS // PART_ROWS) + part
            rows = slice(part * PART_ROWS, (part + 1) * PART_ROWS)
            for tile in range(2):
                pair = jnp.where(odd, odd_pairs[tile][rows], even_pairs[tile][rows])
                heads_out[slot, tile * PART_ROWS : (tile + 1) * PART_ROWS] = pair.astype(
                    jnp.bfloat16
                )
            begin = part * PART_ROWS
            above, below = slice(begin, begin + LANES), slice(begin + LANES, begin + PART_ROWS)
            packed = jnp.where(
                odd,
                jnp.where(near, single_turned[above], single[below]),
                jnp.where(near, single[above], single_turned[below]),
            )
            heads_out[slot, 2 * PART_ROWS :] = packed.astype(jnp.bfloat16)
        return carry

    lax.fori_loop(0, blocks, query_block, 0)

    def idle(slot, carry):
        heads_out[slot] = jnp.zeros((PACKED, LANES), jnp.bfloat16)
        return carry

    parts = QUERY_ROWS // PART_ROWS
    lax.fori_loop(blocks * parts, QUERY_BLOCKS * parts, idle, 0)


def attend(scalars, queries, prior, fresh_rows):
    context = PRIOR_SLOTS + NEW_TOKEN_SLOTS
    vector = pl.BlockSpec(memory_space=pltpu.VMEM)
    return pl.pallas_call(
        attend_kernel,
        out_shape=jax.ShapeDtypeStruct(
            (NEW_TOKEN_SLOTS // PART_ROWS, PACKED, LANES), jnp.bfloat16
        ),
        in_specs=[
            pl.BlockSpec(memory_space=pltpu.SMEM),
            vector,
            pl.BlockSpec(memory_space=pltpu.HBM),
            pl.BlockSpec(memory_space=pl.ANY),
        ],
        out_specs=vector,
        scratch_shapes=[
            pltpu.VMEM((context, WINDOW), jnp.bfloat16),
            pltpu.VMEM((context, WINDOW), jnp.bfloat16),
            pltpu.VMEM((LANES, context), jnp.bfloat16),
            pltpu.VMEM((2, context, LANES), jnp.bfloat16),
            pltpu.VMEM((STACK, LANES), jnp.float32),
            pltpu.VMEM((STACK, LANES), jnp.float32),
            pltpu.SemaphoreType.DMA((2, PRIOR_SLOTS // KEY_ROWS + 1)),
        ],
        compiler_params=pltpu.CompilerParams(vmem_limit_bytes=56 * MIB),
        cost_estimate=pl.CostEstimate(
            flops=4 * 5120 * 7680 * 256, bytes_accessed=12 * MIB, transcendentals=5120 * 7680
        ),
        name="attend",
    )(scalars, queries, prior, fresh_rows)


def finish_kernel(
    scalars,
    heads,
    w_out_hbm,
    hidden_hbm,
    received,
    result,
    decode,
    w_out,
    hidden,
    joined,
    semaphores,
    move_semaphores,
):
    rank, fresh = scalars[2], scalars[1]
    rows = result.shape[0]
    wide = FINISH_COLUMNS
    steps = result.shape[1] // wide
    loads = [
        pltpu.make_async_copy(
            w_out_hbm.at[:, pl.ds(step * wide, wide)], w_out.at[step], semaphores.at[step]
        )
        for step in range(steps)
    ]
    own_rows = pltpu.make_async_copy(
        hidden_hbm.at[pl.ds(pl.multiple_of(rank * rows, rows), rows)], hidden, semaphores.at[steps]
    )
    for copy in loads[:1] + [own_rows] + loads[1:]:
        copy.start()
    moves = [
        pltpu.make_async_copy(
            received.at[pl.ds(part * 8, 8)], decode.at[pl.ds(part * 8, 8)], move_semaphores.at[part]
        )
        for part in range(received.shape[0] // 8)
    ]
    for move in moves:
        move.start()
    low = lane_ids(LANES) < HEAD_SIZE
    for pair in range(2):
        first, second = heads.at[2 * pair], heads.at[2 * pair + 1]
        for tile in range(2):
            source = slice(tile * PART_ROWS, (tile + 1) * PART_ROWS)
            columns = (5 * pair + tile) * LANES
            joined[:, columns : columns + LANES] = first[source]
            joined[:, columns + 3 * LANES : columns + 4 * LANES] = second[source]
        one = first[2 * PART_ROWS :].astype(jnp.float32)
        two = second[2 * PART_ROWS :].astype(jnp.float32)
        columns = (5 * pair + 2) * LANES
        joined[:LANES, columns : columns + LANES] = jnp.where(low, one, two).astype(jnp.bfloat16)
        one, two = pltpu.roll(one, HEAD_SIZE, 1), pltpu.roll(two, HEAD_SIZE, 1)
        joined[LANES:, columns : columns + LANES] = jnp.where(low, one, two).astype(jnp.bfloat16)
    own_rows.wait()
    alive = lax.broadcasted_iota(jnp.int32, (rows, wide), 0) + rank * rows < fresh
    for step in range(steps):
        columns = slice(step * wide, (step + 1) * wide)
        loads[step].wait()
        mixed = jnp.dot(joined[...], w_out[step], preferred_element_type=jnp.float32)
        value = hidden[:, columns].astype(jnp.float32) + mixed
        result[:, columns] = jnp.where(alive, value, 0.0).astype(jnp.bfloat16)
    for move in moves:
        move.wait()


def finish(scalars, heads, w_out, hidden_in, received):
    model = w_out.shape[1]
    vector = pl.BlockSpec(memory_space=pltpu.VMEM)
    far = pl.BlockSpec(memory_space=pltpu.HBM)
    return pl.pallas_call(
        finish_kernel,
        out_shape=(
            jax.ShapeDtypeStruct((PART_ROWS, model), jnp.bfloat16),
            jax.ShapeDtypeStruct(received.shape, received.dtype),
        ),
        in_specs=[pl.BlockSpec(memory_space=pltpu.SMEM), vector, far, far, far],
        out_specs=[vector, far],
        scratch_shapes=[
            pltpu.VMEM((model // FINISH_COLUMNS, w_out.shape[0], FINISH_COLUMNS), jnp.bfloat16),
            pltpu.VMEM((PART_ROWS, model), jnp.bfloat16),
            pltpu.VMEM((PART_ROWS, w_out.shape[0]), jnp.bfloat16),
            pltpu.SemaphoreType.DMA((model // FINISH_COLUMNS + 1,)),
            pltpu.SemaphoreType.DMA((received.shape[0] // 8,)),
        ],
        compiler_params=pltpu.CompilerParams(vmem_limit_bytes=57 * MIB),
        cost_estimate=pl.CostEstimate(
            flops=2 * PART_ROWS * w_out.shape[0] * model,
            bytes_accessed=12 * MIB,
            transcendentals=0,
        ),
        name="finish",
    )(scalars, heads, w_out, hidden_in, received)


def shards(
    hidden_in,
    norm_gain,
    w_query,
    key_value_weight,
    w_out,
    prior_cache,
    cache_len,
    group_len,
    page_map,
):
    rank = lax.axis_index("tp").astype(jnp.int32)
    tp_count = lax.axis_size("tp")
    req_count = lax.axis_size("req")
    scalars = jnp.stack([cache_len[0], group_len[0], rank])

    half_size = HEAD_SIZE // 2
    frequency = 10000.0 ** (-(jnp.arange(half_size, dtype=jnp.float32) * 2.0 / HEAD_SIZE))
    positions = cache_len[0] + jnp.arange(NEW_TOKEN_SLOTS, dtype=jnp.int32)
    angles = positions.astype(jnp.float32)[:, None] * jnp.tile(frequency, 4)[None, :]
    sign = jnp.where(jnp.arange(LANES) % HEAD_SIZE < half_size, -1.0, 1.0)
    cosine = jnp.cos(angles)
    sine = jnp.sin(angles) * sign[None, :]

    targets = jnp.arange(req_count, dtype=jnp.int32) * tp_count + rank
    order = jnp.arange(page_map.shape[1], dtype=jnp.int32)
    picks = jnp.sum(
        jnp.where(page_map[0][None, :] == targets[:, None], order[None, :], 0), axis=1
    ).astype(jnp.int32)

    prior = prior_cache[0]
    queries, keyval = project(hidden_in, norm_gain, w_query, key_value_weight, cosine, sine)
    outgoing = pick_blocks(scalars, picks, prior, keyval)
    outgoing, scalars = lax.optimization_barrier((outgoing, scalars))
    received = lax.all_to_all(outgoing, "req", split_axis=0, concat_axis=0, tiled=True)
    attended = attend(scalars, queries, prior, keyval)
    attended, received = lax.optimization_barrier((attended, received))
    heads = lax.all_to_all(attended, "tp", split_axis=0, concat_axis=0, tiled=True)
    hidden_out, decode_kv = finish(scalars, heads, w_out, hidden_in, received)
    return (hidden_out, decode_kv[None])


def solution(mesh):
    placed = (
        P("req", None),
        P(),
        P(None, "tp"),
        P(),
        P(),
        P("req", None, None),
        P("req"),
        P("req"),
        P("req", None),
    )
    return jax.shard_map(
        shards,
        mesh=mesh,
        in_specs=placed,
        out_specs=(P(("req", "tp"), None), P(("req", "tp"), None, None, None)),
        check_vma=False,
    )
```

time: 156 us -> 192 us (1.23)
  the two profiles are of different devices: /device:TPU:24 before, /device:TPU:12 now
where the time goes in v2:
time: 192 us; the launch traced here: 191 us
  Pallas kernels  161 us (84%)
  blocking collectives  14.2 us (7%)
  starting transfers between devices  7.28 us (4%)
  other arithmetic  5.15 us (3%)
  between operations  2.17 us (1%)
    pallas_call x1, Pallas kernels, finish(): pl.pallas_call(finish_kernel, out_shape=(jax.ShapeDtypeStruct((PART_ROWS,...  82.7 us
    pallas_call x1, Pallas kernels, attend(): pl.pallas_call(attend_kernel, out_shape=jax.ShapeDtypeStruct((NEW_TOKEN_S...  61.8 us
    all_to_all x1, blocking collectives, shards(): lax.all_to_all(attended, 'tp', split_axis=0, concat_axis=0, tiled=True)  14.2 us
    pallas_call x1, Pallas kernels, project(): pl.pallas_call(project_kernel, out_shape=(jax.ShapeDtypeStruct((QUERY_BLO...  12.2 us
    all_to_all x1, starting transfers between devices, shards(): lax.all_to_all(outgoing, 'req', split_axis=0, concat_axis=0, tiled=True)  7.28 us
    pallas_call x1, Pallas kernels, pick_blocks(): pl.pallas_call(pick_kernel, out_shape=jax.ShapeDtypeStruct((count, BLOCK_...  4.2 us
  transfers between devices with their start and end apart: 1, of which 0 were waited for; matrix products, arithmetic and copies ran while one was open for 0% of the time, Pallas kernels for 32%

profile of v2, /device:TPU:12, one launch (start us, length us, event | category | flops | bytes accessed | tf_op | source)
XLA Modules:
  0.0 191.0 jit_solution(494860282511005007)
XLA Ops:
  2.0 0.1 mul.39
  2.1 1.3 reshape.35.gain
  3.4 0.7 pad_add_fusion.scalars
  4.0 1.4 select_reduce_fusion.picks
  5.4 3.0 %fusion = (f32[1024,128]{1,0:T(8,128)}, f32[1024,128]{1,0:T(8,128)}) fusion(f32[128]{0:T(128)S(1)} %compare_select_fusion, f32[128]{0:T(128)S(1)} %mul.39, f32[1024]{0:T(1024)S(1)} %add_convert_fusion), kind=kLoop, calls=%fused_computation.2 | loop fusion | flops 262144 | bytes 1053696 | tf_op jit(solution)/shard_map/mul | solution.py:596
  8.5 12.2 %project.1 = (bf16[2,2560,64]{2,1,0:T(8,128)(2,1)}, bf16[1024,640]{1,0:T(8,128)(2,1)}) custom-call(bf16[1024,2048]{1,0:T(8,128)(2,1)} %hidden_hbm.3, bf16[1,2048]{1,0:T(2,128)(2,1)} %reshape.35.gain, bf16[320,2048]{1,0:T(8,128)(2,1)} %bitcast.10, bf16[2048,640]{1,0:T(8,128)(2,1)} %w_keyval_hbm.1, f32[1024,128]{1,0:T(8,128)} %get-tuple-element.19.cosine, ...), custom_call_target="tpu_custom_call" | custom-call | flops 4026531840 | bytes 10485760 | tf_op jit(solution)/shard_map/project/pallas_call | solution.py:152
  20.7 4.2 %pick_blocks.1 = bf16[32,64,640]{2,1,0:T(8,128)(2,1)} custom-call(s32[3]{0:T(128)} %pad_add_fusion.scalars, s32[32]{0:T(128)} %select_reduce_fusion.picks, bf16[7168,640]{1,0:T(8,128)(2,1)} %bitcast.7, bf16[1024,640]{1,0:T(8,128)(2,1)} %get-tuple-element.10.keyval.fresh_rows), custom_call_target="tpu_custom_call" | custom-call | bytes 5242880 | tf_op jit(solution)/shard_map/pick_blocks/pallas_call | solution.py:228
  24.9 7.3 %all-to-all-start = ((bf16[32,64,640]{2,1,0:T(8,128)(2,1)}), bf16[32,64,640]{2,1,0:T(8,128)(2,1)S(1)}, u32[]{:S(2)}, u32[]{:S(2)}) async-start(bf16[32,64,640]{2,1,0:T(8,128)(2,1)} %pick_blocks.1), calls=%async_computation | async-start | bytes 5242880 | tf_op jit(solution)/shard_map/all_to_all | solution.py:608
  32.2 61.8 %attend.1 = bf16[4,640,128]{2,1,0:T(8,128)(2,1)} custom-call(s32[3]{0:T(128)} %pad_add_fusion.scalars, bf16[2,2560,64]{2,1,0:T(8,128)(2,1)} %get-tuple-element.12.queries, bf16[7168,640]{1,0:T(8,128)(2,1)} %bitcast.8, bf16[1024,640]{1,0:T(8,128)(2,1)} %get-tuple-element.10.keyval.fresh_rows), custom_call_target="tpu_custom_call" | custom-call | flops 40265318400 | bytes 12582912 | tf_op jit(solution)/shard_map/attend/pallas_call | solution.py:453
  94.0 0.0 all-to-all-done.received
  94.0 0.0 copy-start
  94.0 14.2 %all_to_all.10.heads = bf16[4,640,128]{2,1,0:T(8,128)(2,1)} all-to-all(bf16[4,640,128]{2,1,0:T(8,128)(2,1)} %attend.1), channel_id=1, replica_groups=mesh['req'=32,'tp'=4] {'tp'}, dimensions={0} | all-to-all | bytes 1310720 | tf_op jit(solution)/shard_map/all_to_all | solution.py:611
  108.2 0.0 copy-done
  108.2 82.7 %finish.1 = (bf16[256,2048]{1,0:T(8,128)(2,1)}, bf16[32,64,640]{2,1,0:T(8,128)(2,1)}) custom-call(s32[3]{0:T(128)} %pad_add_fusion.scalars, bf16[4,640,128]{2,1,0:T(8,128)(2,1)} %all_to_all.10.heads, bf16[1280,2048]{1,0:T(8,128)(2,1)} %w_out_hbm.1, bf16[1024,2048]{1,0:T(8,128)(2,1)} %hidden_hbm.3, bf16[32,64,640]{2,1,0:T(8,128)(2,1)} %copy-done), custom_call_target="tpu_custom_call" | custom-call | flops 1342177280 | bytes 12582912 | tf_op jit(solution)/shard_map/finish/pallas_call | solution.py:549
  (5 shorter events, 0.0 us)
Async XLA Ops:
  24.9 69.1 %all-to-all-start = ((bf16[32,64,640]{2,1,0:T(8,128)(2,1)}), bf16[32,64,640]{2,1,0:T(8,128)(2,1)S(1)}, u32[]{:S(2)}, u32[]{:S(2)}) async-start(bf16[32,64,640]{2,1,0:T(8,128)(2,1)} %pick_blocks.1), calls=%async_computation | async-start | bytes 5242880 | tf_op jit(solution)/shard_map/all_to_all | solution.py:608
  94.0 14.2 %copy-start = (bf16[32,64,640]{2,1,0:T(8,128)(2,1)}, bf16[32,64,640]{2,1,0:T(8,128)(2,1)S(1)}, u32[]{:S(2)}) copy-start(bf16[32,64,640]{2,1,0:T(8,128)(2,1)S(1)} %all-to-all-done.received) | copy-start | bytes 7864324

commit v3 on v2

--- a/solution.py
+++ b/solution.py
@@ -1,5 +1,6 @@
 import jax
 import jax.numpy as jnp
+import numpy as np
 from jax import lax
 from jax.experimental import pallas as pl
 from jax.experimental.pallas import tpu as pltpu
@@ -16,6 +17,7 @@
 LANES = 128
 WINDOW = 256
 LOCAL = 5
+TP = QUERY_HEAD_COUNT // LOCAL
 QUERY_ROWS = 512
 QUERY_BLOCKS = NEW_TOKEN_SLOTS // QUERY_ROWS
 STACK = LOCAL * QUERY_ROWS
@@ -62,22 +64,31 @@
 
 
 def project_kernel(
+    cache_len,
+    group_len,
+    page_map,
     hidden_hbm,
     gain,
     w_query_hbm,
     w_keyval_hbm,
-    cosine,
-    sine,
+    frequency,
+    prior,
     queries,
     keyval,
+    outgoing,
     hidden,
     w_query,
     w_keyval,
     normed,
     mixed_q,
     mixed_kv,
+    cosine,
+    sine,
     semaphores,
+    block_semaphores,
 ):
+    cached, fresh = cache_len[0], group_len[0]
+    rank = lax.axis_index("tp")
     total = hidden.shape[0]
     pieces = total // NORM_ROWS
     loads = [
@@ -95,12 +106,50 @@
     for copy in loads[:2] + weights + loads[2:]:
         copy.start()
 
+    def prior_copy(block, slot):
+        start = pl.multiple_of(block * BLOCK_ROWS, BLOCK_ROWS)
+        return pltpu.make_async_copy(
+            prior.at[pl.ds(start, BLOCK_ROWS)], outgoing.at[slot], block_semaphores.at[slot]
+        )
+
+    def send(block, carry):
+        device = page_map[0, block]
+        slot = device // TP
+        ours = device % TP == rank
+
+        @pl.when(ours & (block * BLOCK_ROWS < cached))
+        def _():
+            prior_copy(block, slot).start()
+
+        @pl.when(ours & (block * BLOCK_ROWS >= cached))
+        def _():
+            outgoing[slot] = jnp.zeros((BLOCK_ROWS, WIDTH), jnp.bfloat16)
+
+        return carry
+
+    lax.fori_loop(0, PRIOR_SLOTS // BLOCK_ROWS, send, 0)
+
+    count = 32
+    steps = lax.broadcasted_iota(jnp.int32, (count, LANES), 0)
+    coarse = (steps * count + cached).astype(jnp.float32) * frequency[...]
+    fine = steps.astype(jnp.float32) * frequency[...]
+    coarse_cos, coarse_sin = jnp.cos(coarse), jnp.sin(coarse)
+    fine_cos, fine_sin = jnp.cos(fine), jnp.sin(fine)
+    low_half = lane_ids(count) % HEAD_SIZE < HEAD_SIZE // 2
+    for step in range(total // count):
+        here = pl.ds(step * count, count)
+        far_cos, far_sin = coarse_cos[step : step + 1], coarse_sin[step : step + 1]
+        cosine[here] = far_cos * fine_cos - far_sin * fine_sin
+        both = far_sin * fine_cos + far_cos * fine_sin
+        sine[here] = jnp.where(low_half, -both, both)
+
     def norm(piece):
         here = pl.ds(piece * NORM_ROWS, NORM_ROWS)
         value = hidden[here].astype(jnp.float32)
         scale = lax.rsqrt(jnp.mean(value * value, axis=-1, keepdims=True) + 1e-05)
-        normed[here] = (value * scale * gain[...].astype(jnp.float32)).astype(jnp.bfloat16)
-
+        normed[here] = (value * scale * scale_row).astype(jnp.bfloat16)
+
+    scale_row = gain[...].astype(jnp.float32).reshape(1, -1)
     lanes = lane_ids(PROJECT_ROWS)
 
     def mix(block):
@@ -122,15 +171,14 @@
             elif tile == 2:
                 raw = jnp.where(lanes < HEAD_SIZE, rotate(raw, cos, sin), raw)
             keyval[here, columns] = raw.astype(jnp.bfloat16)
-        for head in range(LOCAL):
-            tile = head // 2
+        for tile in range(3):
             raw = mixed_q[here, tile * LANES : (tile + 1) * LANES]
             turned = rotate(raw, cos, sin) * HEAD_SIZE**-0.5
-            if head % 2:
-                turned = pltpu.roll(turned, HEAD_SIZE, 1)
-            queries[block, head * QUERY_ROWS : (head + 1) * QUERY_ROWS] = turned[
-                :, :HEAD_SIZE
-            ].astype(jnp.bfloat16)
+            for head in range(2 * tile, min(2 * tile + 2, LOCAL)):
+                own = turned if head % 2 == 0 else pltpu.roll(turned, HEAD_SIZE, 1)
+                queries[block, head * QUERY_ROWS : (head + 1) * QUERY_ROWS] = own[
+                    :, :HEAD_SIZE
+                ].astype(jnp.bfloat16)
 
     for piece in range(2):
         loads[piece].wait()
@@ -144,9 +192,43 @@
     turn(0)
     turn(1)
 
-
-def project(hidden_in, norm_gain, w_query, w_keyval, cosine, sine):
+    def trim(slot, live, value):
+        rows = lax.broadcasted_iota(jnp.int32, (BLOCK_ROWS, WIDTH), 0)
+        outgoing[slot] = jnp.where(rows < live, value.astype(jnp.float32), 0.0).astype(jnp.bfloat16)
+
+    for block in range(total // BLOCK_ROWS):
+        device = page_map[0, PRIOR_SLOTS // BLOCK_ROWS + block]
+
+        @pl.when(device % TP == rank)
+        def _():
+            trim(device // TP, fresh - block * BLOCK_ROWS, keyval[pl.ds(block * BLOCK_ROWS, BLOCK_ROWS)])
+
+    def receive(block, carry):
+        device = page_map[0, block]
+        slot = device // TP
+        live = cached - block * BLOCK_ROWS
+        ours = (device % TP == rank) & (live > 0)
+
+        @pl.when(ours)
+        def _():
+            prior_copy(block, slot).wait()
+
+        @pl.when(ours & (live < BLOCK_ROWS))
+        def _():
+            trim(slot, live, outgoing[slot])
+
+        return carry
+
+    lax.fori_loop(0, PRIOR_SLOTS // BLOCK_ROWS, receive, 0)
+
+
+def project(cache_len, group_len, page_map, hidden_in, norm_gain, w_query, w_keyval, prior):
     rows, model = hidden_in.shape
+    half_size = HEAD_SIZE // 2
+    frequency = 10000.0 ** (-(np.arange(half_size, dtype=np.float64) * 2.0 / HEAD_SIZE))
+    frequency = jnp.asarray(np.tile(frequency, LANES // half_size)[None].astype(np.float32))
+    count = page_map.shape[1] // TP
+    scalar = pl.BlockSpec(memory_space=pltpu.SMEM)
     vector = pl.BlockSpec(memory_space=pltpu.VMEM)
     far = pl.BlockSpec(memory_space=pltpu.HBM)
     return pl.pallas_call(
@@ -154,9 +236,10 @@
         out_shape=(
             jax.ShapeDtypeStruct((QUERY_BLOCKS, STACK, HEAD_SIZE), jnp.bfloat16),
             jax.ShapeDtypeStruct((rows, WIDTH), jnp.bfloat16),
-        ),
-        in_specs=[far, vector, far, far, vector, vector],
-        out_specs=[vector, vector],
+            jax.ShapeDtypeStruct((count, BLOCK_ROWS, WIDTH), jnp.bfloat16),
+        ),
+        in_specs=[scalar, scalar, scalar, far, vector, far, far, vector, far],
+        out_specs=[vector, vector, vector],
         scratch_shapes=[
             pltpu.VMEM((rows, model), jnp.bfloat16),
             pltpu.VMEM((SPAN, model), jnp.bfloat16),
@@ -164,88 +247,32 @@
             pltpu.VMEM((rows, model), jnp.bfloat16),
             pltpu.VMEM((rows, 3 * LANES), jnp.float32),
             pltpu.VMEM((rows, WIDTH), jnp.float32),
+            pltpu.VMEM((rows, LANES), jnp.float32),
+            pltpu.VMEM((rows, LANES), jnp.float32),
             pltpu.SemaphoreType.DMA((rows // NORM_ROWS + 2,)),
+            pltpu.SemaphoreType.DMA((count,)),
         ],
         compiler_params=pltpu.CompilerParams(vmem_limit_bytes=58 * MIB),
         cost_estimate=pl.CostEstimate(
-            flops=2 * rows * model * (SPAN + WIDTH), bytes_accessed=10 * MIB, transcendentals=0
+            flops=2 * rows * model * (SPAN + WIDTH), bytes_accessed=15 * MIB, transcendentals=0
         ),
         name="project",
-    )(hidden_in, norm_gain.reshape(1, -1), w_query.T, w_keyval, cosine, sine)
-
-
-def pick_kernel(scalars, picks, prior, keyval, outgoing, semaphores):
-    cached, fresh = scalars[0], scalars[1]
-    count = outgoing.shape[0]
-    prior_blocks = PRIOR_SLOTS // BLOCK_ROWS
-
-    def live_rows(block):
-        return jnp.where(
-            block < prior_blocks,
-            cached - block * BLOCK_ROWS,
-            fresh - (block - prior_blocks) * BLOCK_ROWS,
-        )
-
-    for slot in range(count):
-        block = picks[slot]
-
-        @pl.when((block < prior_blocks) & (live_rows(block) > 0))
-        def _():
-            start = pl.multiple_of(block * BLOCK_ROWS, BLOCK_ROWS)
-            pltpu.make_async_copy(
-                prior.at[pl.ds(start, BLOCK_ROWS)], outgoing.at[slot], semaphores.at[slot]
-            ).start()
-
-        @pl.when((block >= prior_blocks) & (live_rows(block) > 0))
-        def _():
-            start = pl.multiple_of((block - prior_blocks) * BLOCK_ROWS, BLOCK_ROWS)
-            pltpu.make_async_copy(
-                keyval.at[pl.ds(start, BLOCK_ROWS)], outgoing.at[slot], semaphores.at[slot]
-            ).start()
-
-    for slot in range(count):
-        live = live_rows(picks[slot])
-
-        @pl.when(live <= 0)
-        def _():
-            outgoing[slot] = jnp.zeros((BLOCK_ROWS, WIDTH), jnp.bfloat16)
-
-        @pl.when(live > 0)
-        def _():
-            pltpu.make_async_copy(
-                prior.at[pl.ds(0, BLOCK_ROWS)], outgoing.at[slot], semaphores.at[slot]
-            ).wait()
-
-        @pl.when((live > 0) & (live < BLOCK_ROWS))
-        def _():
-            rows = lax.broadcasted_iota(jnp.int32, (BLOCK_ROWS, WIDTH), 0)
-            value = outgoing[slot].astype(jnp.float32)
-            outgoing[slot] = jnp.where(rows < live, value, 0.0).astype(jnp.bfloat16)
-
-
-def pick_blocks(scalars, picks, prior, keyval):
-    count = picks.shape[0]
-    return pl.pallas_call(
-        pick_kernel,
-        out_shape=jax.ShapeDtypeStruct((count, BLOCK_ROWS, WIDTH), jnp.bfloat16),
-        grid_spec=pltpu.PrefetchScalarGridSpec(
-            num_scalar_prefetch=2,
-            grid=(1,),
-            in_specs=[
-                pl.BlockSpec(memory_space=pltpu.HBM),
-                pl.BlockSpec(memory_space=pl.ANY),
-            ],
-            out_specs=pl.BlockSpec((count, BLOCK_ROWS, WIDTH), lambda i, s, p: (0, 0, 0)),
-            scratch_shapes=[pltpu.SemaphoreType.DMA((count,))],
-        ),
-        compiler_params=pltpu.CompilerParams(vmem_limit_bytes=56 * MIB),
-        cost_estimate=pl.CostEstimate(flops=0, bytes_accessed=5 * MIB, transcendentals=0),
-        name="pick_blocks",
-    )(scalars, picks, prior, keyval)
+    )(
+        cache_len,
+        group_len,
+        page_map,
+        hidden_in,
+        norm_gain,
+        w_query.T,
+        w_keyval,
+        frequency,
+        prior,
+    )
 
 
 def attend_kernel(
-    scalars,
+    cache_len,
+    group_len,
     queries,
     prior,
     fresh_rows,
@@ -258,7 +285,7 @@
     total,
     semaphores,
 ):
-    cached, fresh, rank = scalars[0], scalars[1], scalars[2]
+    cached, fresh, rank = cache_len[0], group_len[0], lax.axis_index("tp")
     key_start = pl.multiple_of(key_tile_start(rank) * LANES, LANES)
     value_start = pl.multiple_of(value_tile_start(rank) * LANES, LANES)
     key_shift, value_shift = key_offset(rank), value_offset(rank)
@@ -447,7 +474,7 @@
     lax.fori_loop(blocks * parts, QUERY_BLOCKS * parts, idle, 0)
 
 
-def attend(scalars, queries, prior, fresh_rows):
+def attend(cache_len, group_len, queries, prior, fresh_rows):
     context = PRIOR_SLOTS + NEW_TOKEN_SLOTS
     vector = pl.BlockSpec(memory_space=pltpu.VMEM)
     return pl.pallas_call(
@@ -456,6 +483,7 @@
             (NEW_TOKEN_SLOTS // PART_ROWS, PACKED, LANES), jnp.bfloat16
         ),
         in_specs=[
+            pl.BlockSpec(memory_space=pltpu.SMEM),
             pl.BlockSpec(memory_space=pltpu.SMEM),
             vector,
             pl.BlockSpec(memory_space=pltpu.HBM),
@@ -476,11 +504,11 @@
             flops=4 * 5120 * 7680 * 256, bytes_accessed=12 * MIB, transcendentals=5120 * 7680
         ),
         name="attend",
-    )(scalars, queries, prior, fresh_rows)
+    )(cache_len, group_len, queries, prior, fresh_rows)
 
 
 def finish_kernel(
-    scalars,
+    group_len,
     heads,
     w_out_hbm,
     hidden_hbm,
@@ -490,10 +518,11 @@
     w_out,
     hidden,
     joined,
+    passing,
     semaphores,
     move_semaphores,
 ):
-    rank, fresh = scalars[2], scalars[1]
+    rank, fresh = lax.axis_index("tp"), group_len[0]
     rows = result.shape[0]
     wide = FINISH_COLUMNS
     steps = result.shape[1] // wide
@@ -508,14 +537,19 @@
     )
     for copy in loads[:1] + [own_rows] + loads[1:]:
         copy.start()
-    moves = [
-        pltpu.make_async_copy(
-            received.at[pl.ds(part * 8, 8)], decode.at[pl.ds(part * 8, 8)], move_semaphores.at[part]
-        )
-        for part in range(received.shape[0] // 8)
-    ]
-    for move in moves:
-        move.start()
+    pieces = move_semaphores.shape[1]
+    slots = received.shape[0] // pieces
+    fetches, stores = [], []
+    for piece in range(pieces):
+        here = pl.ds(piece * slots, slots)
+        fetches.append(
+            pltpu.make_async_copy(received.at[here], passing.at[here], move_semaphores.at[0, piece])
+        )
+        stores.append(
+            pltpu.make_async_copy(passing.at[here], decode.at[here], move_semaphores.at[1, piece])
+        )
+    for copy in fetches:
+        copy.start()
     low = lane_ids(LANES) < HEAD_SIZE
     for pair in range(2):
         first, second = heads.at[2 * pair], heads.at[2 * pair + 1]
@@ -530,6 +564,9 @@
         joined[:LANES, columns : columns + LANES] = jnp.where(low, one, two).astype(jnp.bfloat16)
         one, two = pltpu.roll(one, HEAD_SIZE, 1), pltpu.roll(two, HEAD_SIZE, 1)
         joined[LANES:, columns : columns + LANES] = jnp.where(low, one, two).astype(jnp.bfloat16)
+    for fetch, store in zip(fetches, stores):
+        fetch.wait()
+        store.start()
     own_rows.wait()
     alive = lax.broadcasted_iota(jnp.int32, (rows, wide), 0) + rank * rows < fresh
     for step in range(steps):
@@ -538,11 +575,11 @@
         mixed = jnp.dot(joined[...], w_out[step], preferred_element_type=jnp.float32)
         value = hidden[:, columns].astype(jnp.float32) + mixed
         result[:, columns] = jnp.where(alive, value, 0.0).astype(jnp.bfloat16)
-    for move in moves:
-        move.wait()
-
-
-def finish(scalars, heads, w_out, hidden_in, received):
+    for store in stores:
+        store.wait()
+
+
+def finish(group_len, heads, w_out, hidden_in, received):
     model = w_out.shape[1]
     vector = pl.BlockSpec(memory_space=pltpu.VMEM)
     far = pl.BlockSpec(memory_space=pltpu.HBM)
@@ -558,17 +595,18 @@
             pltpu.VMEM((model // FINISH_COLUMNS, w_out.shape[0], FINISH_COLUMNS), jnp.bfloat16),
             pltpu.VMEM((PART_ROWS, model), jnp.bfloat16),
             pltpu.VMEM((PART_ROWS, w_out.shape[0]), jnp.bfloat16),
+            pltpu.VMEM(received.shape, received.dtype),
             pltpu.SemaphoreType.DMA((model // FINISH_COLUMNS + 1,)),
-            pltpu.SemaphoreType.DMA((received.shape[0] // 8,)),
+            pltpu.SemaphoreType.DMA((2, 4)),
         ],
-        compiler_params=pltpu.CompilerParams(vmem_limit_bytes=57 * MIB),
+        compiler_params=pltpu.CompilerParams(vmem_limit_bytes=58 * MIB),
         cost_estimate=pl.CostEstimate(
             flops=2 * PART_ROWS * w_out.shape[0] * model,
             bytes_accessed=12 * MIB,
             transcendentals=0,
         ),
         name="finish",
-    )(scalars, heads, w_out, hidden_in, received)
+    )(group_len, heads, w_out, hidden_in, received)
 
 
 def shards(
@@ -582,34 +620,16 @@
     group_len,
     page_map,
 ):
-    rank = lax.axis_index("tp").astype(jnp.int32)
-    tp_count = lax.axis_size("tp")
-    req_count = lax.axis_size("req")
-    scalars = jnp.stack([cache_len[0], group_len[0], rank])
-
-    half_size = HEAD_SIZE // 2
-    frequency = 10000.0 ** (-(jnp.arange(half_size, dtype=jnp.float32) * 2.0 / HEAD_SIZE))
-    positions = cache_len[0] + jnp.arange(NEW_TOKEN_SLOTS, dtype=jnp.int32)
-    angles = positions.astype(jnp.float32)[:, None] * jnp.tile(frequency, 4)[None, :]
-    sign = jnp.where(jnp.arange(LANES) % HEAD_SIZE < half_size, -1.0, 1.0)
-    cosine = jnp.cos(angles)
-    sine = jnp.sin(angles) * sign[None, :]
-
-    targets = jnp.arange(req_count, dtype=jnp.int32) * tp_count + rank
-    order = jnp.arange(page_map.shape[1], dtype=jnp.int32)
-    picks = jnp.sum(
-        jnp.where(page_map[0][None, :] == targets[:, None], order[None, :], 0), axis=1
-    ).astype(jnp.int32)
-
     prior = prior_cache[0]
-    queries, keyval = project(hidden_in, norm_gain, w_query, key_value_weight, cosine, sine)
-    outgoing = pick_blocks(scalars, picks, prior, keyval)
-    outgoing, scalars = lax.optimization_barrier((outgoing, scalars))
+    queries, keyval, outgoing = project(
+        cache_len, group_len, page_map, hidden_in, norm_gain, w_query, key_value_weight, prior
+    )
+    outgoing, queries = lax.optimization_barrier((outgoing, queries))
     received = lax.all_to_all(outgoing, "req", split_axis=0, concat_axis=0, tiled=True)
-    attended = attend(scalars, queries, prior, keyval)
+    attended = attend(cache_len, group_len, queries, prior, keyval)
     attended, received = lax.optimization_barrier((attended, received))
     heads = lax.all_to_all(attended, "tp", split_axis=0, concat_axis=0, tiled=True)
-    hidden_out, decode_kv = finish(scalars, heads, w_out, hidden_in, received)
+    hidden_out, decode_kv = finish(group_len, heads, w_out, hidden_in, received)
     return (hidden_out, decode_kv[None])
 
 

time: 192 us -> 110 us (0.57)
  the two profiles are of different devices: /device:TPU:12 before, /device:TPU:31 now
where the time goes in v3:
time: 110 us; the launch traced here: 109 us
  Pallas kernels  86 us (78%)
  blocking collectives  12.8 us (12%)
  starting transfers between devices  7.67 us (7%)
  between operations  2.12 us (2%)
    pallas_call x1, Pallas kernels, attend(): pl.pallas_call(attend_kernel, out_shape=jax.ShapeDtypeStruct((NEW_TOKEN_S...  61.8 us
    pallas_call x1, Pallas kernels, project(): pl.pallas_call(project_kernel, out_shape=(jax.ShapeDtypeStruct((QUERY_BLO...  15.8 us
    all_to_all x1, blocking collectives, shards(): lax.all_to_all(attended, 'tp', split_axis=0, concat_axis=0, tiled=True)  12.8 us
    pallas_call x1, Pallas kernels, finish(): pl.pallas_call(finish_kernel, out_shape=(jax.ShapeDtypeStruct((PART_ROWS,...  8.35 us
    all_to_all x1, starting transfers between devices, shards(): lax.all_to_all(outgoing, 'req', split_axis=0, concat_axis=0, tiled=True)  7.67 us
  transfers between devices with their start and end apart: 1, of which 0 were waited for; matrix products, arithmetic and copies ran while one was open for 0% of the time, Pallas kernels for 57%

profile of v3, /device:TPU:31, one launch (start us, length us, event | category | flops | bytes accessed | tf_op | source)
XLA Modules:
  0.0 108.6 jit_solution(11468404590939661499)
XLA Ops:
  1.9 15.8 %project.1 = (bf16[2,2560,64]{2,1,0:T(8,128)(2,1)}, bf16[1024,640]{1,0:T(8,128)(2,1)}, bf16[32,64,640]{2,1,0:T(8,128)(2,1)}) custom-call(s32[1]{0:T(128)S(6)} %copy.12.cache_len, s32[1]{0:T(128)S(6)} %copy.13.group_len, s32[1,128]{1,0:T(1,128)} %page_map.1, bf16[1024,2048]{1,0:T(8,128)(2,1)} %hidden_hbm.3, bf16[2048]{0:T(1024)(128)(2,1)} %gain.1, ...), custom_call_target="tpu_custom_call" | custom-call | flops 4026531840 | bytes 15728640 | tf_op jit(solution)/shard_map/project/pallas_call | solution.py:234
  17.8 7.7 %all-to-all-start = ((bf16[32,64,640]{2,1,0:T(8,128)(2,1)}), bf16[32,64,640]{2,1,0:T(8,128)(2,1)S(1)}, u32[]{:S(2)}, u32[]{:S(2)}) async-start(bf16[32,64,640]{2,1,0:T(8,128)(2,1)} %get-tuple-element.15), calls=%async_computation | async-start | bytes 5242880 | tf_op jit(solution)/shard_map/all_to_all | solution.py:628
  25.4 61.8 %attend.1 = bf16[4,640,128]{2,1,0:T(8,128)(2,1)} custom-call(s32[1]{0:T(128)S(6)} %copy.12.cache_len, s32[1]{0:T(128)S(6)} %copy.13.group_len, bf16[2,2560,64]{2,1,0:T(8,128)(2,1)} %get-tuple-element.13.queries, bf16[7168,640]{1,0:T(8,128)(2,1)} %bitcast.4, bf16[1024,640]{1,0:T(8,128)(2,1)} %get-tuple-element.14.fresh_rows), custom_call_target="tpu_custom_call" | custom-call | flops 40265318400 | bytes 12582912 | tf_op jit(solution)/shard_map/attend/pallas_call | solution.py:480
  87.2 0.0 all-to-all-done.received
  87.2 0.0 copy-start
  87.3 12.8 %all_to_all.10.heads = bf16[4,640,128]{2,1,0:T(8,128)(2,1)} all-to-all(bf16[4,640,128]{2,1,0:T(8,128)(2,1)} %attend.1), channel_id=1, replica_groups=mesh['req'=32,'tp'=4] {'tp'}, dimensions={0} | all-to-all | bytes 1310720 | tf_op jit(solution)/shard_map/all_to_all | solution.py:631
  100.0 0.0 copy-done
  100.0 8.4 %finish.1 = (bf16[256,2048]{1,0:T(8,128)(2,1)}, bf16[32,64,640]{2,1,0:T(8,128)(2,1)}) custom-call(s32[1]{0:T(128)S(6)} %copy.13.group_len, bf16[4,640,128]{2,1,0:T(8,128)(2,1)} %all_to_all.10.heads, bf16[1280,2048]{1,0:T(8,128)(2,1)} %w_out_hbm.1, bf16[1024,2048]{1,0:T(8,128)(2,1)} %hidden_hbm.3, bf16[32,64,640]{2,1,0:T(8,128)(2,1)} %copy-done), custom_call_target="tpu_custom_call" | custom-call | flops 1342177280 | bytes 12582912 | tf_op jit(solution)/shard_map/finish/pallas_call | solution.py:586
Async XLA Ops:
  17.8 69.5 %all-to-all-start = ((bf16[32,64,640]{2,1,0:T(8,128)(2,1)}), bf16[32,64,640]{2,1,0:T(8,128)(2,1)S(1)}, u32[]{:S(2)}, u32[]{:S(2)}) async-start(bf16[32,64,640]{2,1,0:T(8,128)(2,1)} %get-tuple-element.15), calls=%async_computation | async-start | bytes 5242880 | tf_op jit(solution)/shard_map/all_to_all | solution.py:628
  87.2 12.8 %copy-start = (bf16[32,64,640]{2,1,0:T(8,128)(2,1)}, bf16[32,64,640]{2,1,0:T(8,128)(2,1)S(1)}, u32[]{:S(2)}) copy-start(bf16[32,64,640]{2,1,0:T(8,128)(2,1)S(1)} %all-to-all-done.received) | copy-start | bytes 7864324

commit v4 on v3

--- a/solution.py
+++ b/solution.py
@@ -18,15 +18,19 @@
 WINDOW = 256
 LOCAL = 5
 TP = QUERY_HEAD_COUNT // LOCAL
+TP_BITS = TP.bit_length() - 1
+KEPT = 1 << 20
 QUERY_ROWS = 512
 QUERY_BLOCKS = NEW_TOKEN_SLOTS // QUERY_ROWS
 STACK = LOCAL * QUERY_ROWS
-KEY_ROWS = 1024
+KEY_ROWS = 1792
 PREPARE_ROWS = 256
 PROJECT_ROWS = 512
 NORM_ROWS = 256
 PART_ROWS = 256
 FINISH_COLUMNS = 512
+FINISH_LIMIT = 24
+STORE_LIMIT = 24
 PACKED = PART_ROWS * LOCAL // 2
 BLOCK_ROWS = 64
 MIB = 1 << 20
@@ -73,9 +77,13 @@
     w_keyval_hbm,
     frequency,
     prior,
+    queries_hbm,
+    keyval_hbm,
+    outgoing_hbm,
     queries,
     keyval,
     outgoing,
+    live_rows,
     hidden,
     w_query,
     w_keyval,
@@ -86,6 +94,8 @@
     sine,
     semaphores,
     block_semaphores,
+    store_semaphores,
+    result_semaphores,
 ):
     cached, fresh = cache_len[0], group_len[0]
     rank = lax.axis_index("tp")
@@ -112,22 +122,34 @@
             prior.at[pl.ds(start, BLOCK_ROWS)], outgoing.at[slot], block_semaphores.at[slot]
         )
 
+    def block_store(slot):
+        return pltpu.make_async_copy(
+            outgoing.at[slot], outgoing_hbm.at[slot], store_semaphores.at[slot]
+        )
+
     def send(block, carry):
         device = page_map[0, block]
-        slot = device // TP
-        ours = device % TP == rank
-
-        @pl.when(ours & (block * BLOCK_ROWS < cached))
-        def _():
-            prior_copy(block, slot).start()
-
-        @pl.when(ours & (block * BLOCK_ROWS >= cached))
-        def _():
-            outgoing[slot] = jnp.zeros((BLOCK_ROWS, WIDTH), jnp.bfloat16)
+
+        @pl.when(device & (TP - 1) == rank)
+        def _():
+            slot = device >> TP_BITS
+            live = cached - block * BLOCK_ROWS
+            live_rows[slot] = live
+
+            @pl.when(live > 0)
+            def _():
+                prior_copy(block, slot).start()
 
         return carry
 
-    lax.fori_loop(0, PRIOR_SLOTS // BLOCK_ROWS, send, 0)
+    prior_blocks = PRIOR_SLOTS // BLOCK_ROWS
+    lax.fori_loop(0, prior_blocks, send, 0, unroll=8)
+    for block in range(total // BLOCK_ROWS):
+        device = page_map[0, prior_blocks + block]
+
+        @pl.when(device & (TP - 1) == rank)
+        def _():
+            live_rows[device >> TP_BITS] = KEPT
 
     count = 32
     steps = lax.broadcasted_iota(jnp.int32, (count, LANES), 0)
@@ -180,6 +202,42 @@
                     :, :HEAD_SIZE
                 ].astype(jnp.bfloat16)
 
+    def trim(slot, live, value):
+        rows = lax.broadcasted_iota(jnp.int32, (BLOCK_ROWS, WIDTH), 0)
+        outgoing[slot] = jnp.where(rows < live, value.astype(jnp.float32), 0.0).astype(jnp.bfloat16)
+
+    def forward(slot, carry):
+        live = live_rows[slot]
+
+        @pl.when((live > 0) & (live < KEPT))
+        def _():
+            prior_copy(0, slot).wait()
+
+        @pl.when((live > 0) & (live < BLOCK_ROWS))
+        def _():
+            trim(slot, live, outgoing[slot])
+
+        @pl.when(live <= 0)
+        def _():
+            outgoing[slot] = jnp.zeros((BLOCK_ROWS, WIDTH), jnp.bfloat16)
+
+        @pl.when(live < KEPT)
+        def _():
+            block_store(slot).start()
+
+        return carry
+
+    def result_stores(block):
+        here = pl.ds(block * PROJECT_ROWS, PROJECT_ROWS)
+        return [
+            pltpu.make_async_copy(
+                keyval.at[here], keyval_hbm.at[here], result_semaphores.at[0, block]
+            ),
+            pltpu.make_async_copy(
+                queries.at[block], queries_hbm.at[block], result_semaphores.at[1, block]
+            ),
+        ]
+
     for piece in range(2):
         loads[piece].wait()
         norm(piece)
@@ -188,38 +246,29 @@
     mix(0)
     norm(2)
     norm(3)
+    lax.fori_loop(0, outgoing.shape[0], forward, 0, unroll=4)
     mix(1)
     turn(0)
+    for copy in result_stores(0):
+        copy.start()
     turn(1)
-
-    def trim(slot, live, value):
-        rows = lax.broadcasted_iota(jnp.int32, (BLOCK_ROWS, WIDTH), 0)
-        outgoing[slot] = jnp.where(rows < live, value.astype(jnp.float32), 0.0).astype(jnp.bfloat16)
-
+    for copy in result_stores(1):
+        copy.start()
     for block in range(total // BLOCK_ROWS):
-        device = page_map[0, PRIOR_SLOTS // BLOCK_ROWS + block]
-
-        @pl.when(device % TP == rank)
-        def _():
-            trim(device // TP, fresh - block * BLOCK_ROWS, keyval[pl.ds(block * BLOCK_ROWS, BLOCK_ROWS)])
-
-    def receive(block, carry):
-        device = page_map[0, block]
-        slot = device // TP
-        live = cached - block * BLOCK_ROWS
-        ours = (device % TP == rank) & (live > 0)
-
-        @pl.when(ours)
-        def _():
-            prior_copy(block, slot).wait()
-
-        @pl.when(ours & (live < BLOCK_ROWS))
-        def _():
-            trim(slot, live, outgoing[slot])
-
-        return carry
-
-    lax.fori_loop(0, PRIOR_SLOTS // BLOCK_ROWS, receive, 0)
+        device = page_map[0, prior_blocks + block]
+
+        @pl.when(device & (TP - 1) == rank)
+        def _():
+            slot = device >> TP_BITS
+            rows = keyval[pl.ds(block * BLOCK_ROWS, BLOCK_ROWS)]
+            trim(slot, fresh - block * BLOCK_ROWS, rows)
+            block_store(slot).start()
+
+    for slot in range(outgoing.shape[0]):
+        block_store(slot).wait()
+    for block in range(total // PROJECT_ROWS):
+        for copy in result_stores(block):
+            copy.wait()
 
 
 def project(cache_len, group_len, page_map, hidden_in, norm_gain, w_query, w_keyval, prior):
@@ -239,8 +288,12 @@
             jax.ShapeDtypeStruct((count, BLOCK_ROWS, WIDTH), jnp.bfloat16),
         ),
         in_specs=[scalar, scalar, scalar, far, vector, far, far, vector, far],
-        out_specs=[vector, vector, vector],
+        out_specs=[far, far, far],
         scratch_shapes=[
+            pltpu.VMEM((QUERY_BLOCKS, STACK, HEAD_SIZE), jnp.bfloat16),
+            pltpu.VMEM((rows, WIDTH), jnp.bfloat16),
+            pltpu.VMEM((count, BLOCK_ROWS, WIDTH), jnp.bfloat16),
+            pltpu.SMEM((count,), jnp.int32),
             pltpu.VMEM((rows, model), jnp.bfloat16),
             pltpu.VMEM((SPAN, model), jnp.bfloat16),
             pltpu.VMEM((model, WIDTH), jnp.bfloat16),
@@ -251,6 +304,8 @@
             pltpu.VMEM((rows, LANES), jnp.float32),
             pltpu.SemaphoreType.DMA((rows // NORM_ROWS + 2,)),
             pltpu.SemaphoreType.DMA((count,)),
+            pltpu.SemaphoreType.DMA((count,)),
+            pltpu.SemaphoreType.DMA((2, rows // PROJECT_ROWS)),
         ],
         compiler_params=pltpu.CompilerParams(vmem_limit_bytes=58 * MIB),
         cost_estimate=pl.CostEstimate(
@@ -273,10 +328,11 @@
 def attend_kernel(
     cache_len,
     group_len,
-    queries,
+    queries_hbm,
     prior,
     fresh_rows,
     heads_out,
+    queries,
     raw_keys,
     raw_values,
     keys,
@@ -320,6 +376,9 @@
             raw_values.at[into],
             semaphores.at[1, chunk_limit],
         ),
+    )
+    fresh_copies += (
+        pltpu.make_async_copy(queries_hbm, queries, semaphores.at[0, chunk_limit + 1]),
     )
     for copy in fresh_copies:
         copy.start()
@@ -485,19 +544,20 @@
         in_specs=[
             pl.BlockSpec(memory_space=pltpu.SMEM),
             pl.BlockSpec(memory_space=pltpu.SMEM),
-            vector,
+            pl.BlockSpec(memory_space=pl.ANY),
             pl.BlockSpec(memory_space=pltpu.HBM),
             pl.BlockSpec(memory_space=pl.ANY),
         ],
         out_specs=vector,
         scratch_shapes=[
+            pltpu.VMEM(queries.shape, queries.dtype),
             pltpu.VMEM((context, WINDOW), jnp.bfloat16),
             pltpu.VMEM((context, WINDOW), jnp.bfloat16),
             pltpu.VMEM((LANES, context), jnp.bfloat16),
             pltpu.VMEM((2, context, LANES), jnp.bfloat16),
             pltpu.VMEM((STACK, LANES), jnp.float32),
             pltpu.VMEM((STACK, LANES), jnp.float32),
-            pltpu.SemaphoreType.DMA((2, PRIOR_SLOTS // KEY_ROWS + 1)),
+            pltpu.SemaphoreType.DMA((2, PRIOR_SLOTS // KEY_ROWS + 2)),
         ],
         compiler_params=pltpu.CompilerParams(vmem_limit_bytes=56 * MIB),
         cost_estimate=pl.CostEstimate(
@@ -507,49 +567,48 @@
     )(cache_len, group_len, queries, prior, fresh_rows)
 
 
-def finish_kernel(
-    group_len,
-    heads,
-    w_out_hbm,
-    hidden_hbm,
-    received,
-    result,
-    decode,
-    w_out,
-    hidden,
-    joined,
-    passing,
-    semaphores,
-    move_semaphores,
-):
+def store_kernel(received, w_out, hidden, decode, w_near, hidden_near, semaphores):
+    rows = hidden_near.shape[0]
+    begin = pl.multiple_of(lax.axis_index("tp") * rows, rows)
+    copies = (
+        pltpu.make_async_copy(w_out, w_near, semaphores.at[0]),
+        pltpu.make_async_copy(received, decode, semaphores.at[1]),
+        pltpu.make_async_copy(hidden.at[pl.ds(begin, rows)], hidden_near, semaphores.at[2]),
+    )
+    for copy in copies:
+        copy.start()
+    for copy in copies:
+        copy.wait()
+
+
+def store_blocks(received, w_out, hidden_in):
+    vector = pl.BlockSpec(memory_space=pltpu.VMEM)
+    far = pl.BlockSpec(memory_space=pltpu.HBM)
+    return pl.pallas_call(
+        store_kernel,
+        out_shape=(
+            jax.ShapeDtypeStruct(received.shape, received.dtype),
+            jax.ShapeDtypeStruct(w_out.shape, w_out.dtype),
+            jax.ShapeDtypeStruct((PART_ROWS, hidden_in.shape[1]), hidden_in.dtype),
+        ),
+        in_specs=[vector, far, far],
+        out_specs=[far, vector, vector],
+        scratch_shapes=[pltpu.SemaphoreType.DMA((3,))],
+        compiler_params=pltpu.CompilerParams(vmem_limit_bytes=STORE_LIMIT * MIB),
+        cost_estimate=pl.CostEstimate(flops=0, bytes_accessed=12 * MIB, transcendentals=0),
+        name="store_blocks",
+    )(received, w_out, hidden_in)
+
+
+def finish_kernel(group_len, own, *rest):
+    travelled = rest[: TP - 1]
+    w_out, hidden, result, heads, joined = rest[TP - 1 :]
     rank, fresh = lax.axis_index("tp"), group_len[0]
     rows = result.shape[0]
     wide = FINISH_COLUMNS
     steps = result.shape[1] // wide
-    loads = [
-        pltpu.make_async_copy(
-            w_out_hbm.at[:, pl.ds(step * wide, wide)], w_out.at[step], semaphores.at[step]
-        )
-        for step in range(steps)
-    ]
-    own_rows = pltpu.make_async_copy(
-        hidden_hbm.at[pl.ds(pl.multiple_of(rank * rows, rows), rows)], hidden, semaphores.at[steps]
-    )
-    for copy in loads[:1] + [own_rows] + loads[1:]:
-        copy.start()
-    pieces = move_semaphores.shape[1]
-    slots = received.shape[0] // pieces
-    fetches, stores = [], []
-    for piece in range(pieces):
-        here = pl.ds(piece * slots, slots)
-        fetches.append(
-            pltpu.make_async_copy(received.at[here], passing.at[here], move_semaphores.at[0, piece])
-        )
-        stores.append(
-            pltpu.make_async_copy(passing.at[here], decode.at[here], move_semaphores.at[1, piece])
-        )
-    for copy in fetches:
-        copy.start()
+    for shift, source in enumerate((own,) + tuple(travelled)):
+        heads[(rank + TP - shift) & (TP - 1)] = source[...]
     low = lane_ids(LANES) < HEAD_SIZE
     for pair in range(2):
         first, second = heads.at[2 * pair], heads.at[2 * pair + 1]
@@ -564,49 +623,34 @@
         joined[:LANES, columns : columns + LANES] = jnp.where(low, one, two).astype(jnp.bfloat16)
         one, two = pltpu.roll(one, HEAD_SIZE, 1), pltpu.roll(two, HEAD_SIZE, 1)
         joined[LANES:, columns : columns + LANES] = jnp.where(low, one, two).astype(jnp.bfloat16)
-    for fetch, store in zip(fetches, stores):
-        fetch.wait()
-        store.start()
-    own_rows.wait()
     alive = lax.broadcasted_iota(jnp.int32, (rows, wide), 0) + rank * rows < fresh
     for step in range(steps):
         columns = slice(step * wide, (step + 1) * wide)
-        loads[step].wait()
-        mixed = jnp.dot(joined[...], w_out[step], preferred_element_type=jnp.float32)
+        mixed = jnp.dot(joined[...], w_out[:, columns], preferred_element_type=jnp.float32)
         value = hidden[:, columns].astype(jnp.float32) + mixed
         result[:, columns] = jnp.where(alive, value, 0.0).astype(jnp.bfloat16)
-    for store in stores:
-        store.wait()
-
-
-def finish(group_len, heads, w_out, hidden_in, received):
+
+
+def finish(group_len, heads, w_out, hidden):
     model = w_out.shape[1]
     vector = pl.BlockSpec(memory_space=pltpu.VMEM)
-    far = pl.BlockSpec(memory_space=pltpu.HBM)
     return pl.pallas_call(
         finish_kernel,
-        out_shape=(
-            jax.ShapeDtypeStruct((PART_ROWS, model), jnp.bfloat16),
-            jax.ShapeDtypeStruct(received.shape, received.dtype),
-        ),
-        in_specs=[pl.BlockSpec(memory_space=pltpu.SMEM), vector, far, far, far],
-        out_specs=[vector, far],
+        out_shape=jax.ShapeDtypeStruct((PART_ROWS, model), jnp.bfloat16),
+        in_specs=[pl.BlockSpec(memory_space=pltpu.SMEM)] + [vector] * (TP + 2),
+        out_specs=vector,
         scratch_shapes=[
-            pltpu.VMEM((model // FINISH_COLUMNS, w_out.shape[0], FINISH_COLUMNS), jnp.bfloat16),
-            pltpu.VMEM((PART_ROWS, model), jnp.bfloat16),
+            pltpu.VMEM((TP, PACKED, LANES), jnp.bfloat16),
             pltpu.VMEM((PART_ROWS, w_out.shape[0]), jnp.bfloat16),
-            pltpu.VMEM(received.shape, received.dtype),
-            pltpu.SemaphoreType.DMA((model // FINISH_COLUMNS + 1,)),
-            pltpu.SemaphoreType.DMA((2, 4)),
         ],
-        compiler_params=pltpu.CompilerParams(vmem_limit_bytes=58 * MIB),
+        compiler_params=pltpu.CompilerParams(vmem_limit_bytes=FINISH_LIMIT * MIB),
         cost_estimate=pl.CostEstimate(
             flops=2 * PART_ROWS * w_out.shape[0] * model,
-            bytes_accessed=12 * MIB,
+            bytes_accessed=8 * MIB,
             transcendentals=0,
         ),
         name="finish",
-    )(group_len, heads, w_out, hidden_in, received)
+    )(group_len, *heads, w_out, hidden)
 
 
 def shards(
@@ -628,8 +672,14 @@
     received = lax.all_to_all(outgoing, "req", split_axis=0, concat_axis=0, tiled=True)
     attended = attend(cache_len, group_len, queries, prior, keyval)
     attended, received = lax.optimization_barrier((attended, received))
-    heads = lax.all_to_all(attended, "tp", split_axis=0, concat_axis=0, tiled=True)
-    hidden_out, decode_kv = finish(group_len, heads, w_out, hidden_in, received)
+    rank = lax.axis_index("tp")
+    heads = [lax.dynamic_index_in_dim(attended, rank, 0, keepdims=False)]
+    for shift in range(1, TP):
+        part = lax.dynamic_index_in_dim(attended, (rank + shift) % TP, 0, keepdims=False)
+        pairs = [(source, (source + shift) % TP) for source in range(TP)]
+        heads.append(lax.ppermute(part, "tp", pairs))
+    decode_kv, w_near, hidden_near = store_blocks(received, w_out, hidden_in)
+    hidden_out = finish(group_len, heads, w_near, hidden_near)
     return (hidden_out, decode_kv[None])
 
 

time: 110 us -> 101 us (0.918)
  the two profiles are of different devices: /device:TPU:31 before, /device:TPU:24 now
where the time goes in v4:
time: 101 us; the launch traced here: 99 us
  Pallas kernels  77.8 us (77%)
  starting transfers between devices  12.7 us (13%)
  local copies, waits for them, and re-layouts  5.88 us (6%)
  between operations  2.03 us (2%)
    pallas_call x1, Pallas kernels, attend(): pl.pallas_call(attend_kernel, out_shape=jax.ShapeDtypeStruct((NEW_TOKEN_S...  59.6 us
    pallas_call x1, Pallas kernels, project(): pl.pallas_call(project_kernel, out_shape=(jax.ShapeDtypeStruct((QUERY_BLO...  13.7 us
    all_to_all x1, starting transfers between devices, shards(): lax.all_to_all(outgoing, 'req', split_axis=0, concat_axis=0, tiled=True)  7.43 us
    ppermute x3, starting transfers between devices, shards(): heads.append(lax.ppermute(part, 'tp', pairs))  5.28 us
    unnamed x4, local copies, waits for them, and re-layouts  4.67 us
    pallas_call x1, Pallas kernels, finish(): pl.pallas_call(finish_kernel, out_shape=jax.ShapeDtypeStruct((PART_ROWS,...  2.64 us
  transfers between devices with their start and end apart: 4, of which 1 were waited for; matrix products, arithmetic and copies ran while one was open for 0% of the time, Pallas kernels for 62%

profile of v4, /device:TPU:24, one launch (start us, length us, event | category | flops | bytes accessed | tf_op | source)
XLA Modules:
  0.0 99.0 jit_solution(8357241693991547905)
XLA Ops:
  1.9 13.7 %project.1 = (bf16[2,2560,64]{2,1,0:T(8,128)(2,1)}, bf16[1024,640]{1,0:T(8,128)(2,1)}, bf16[32,64,640]{2,1,0:T(8,128)(2,1)}) custom-call(s32[1]{0:T(128)S(6)} %copy.12.cache_len, s32[1]{0:T(128)S(6)} %copy.13.group_len, s32[1,128]{1,0:T(1,128)} %page_map.1, bf16[1024,2048]{1,0:T(8,128)(2,1)} %hidden.1, bf16[2048]{0:T(1024)(128)(2,1)} %gain.1, ...), custom_call_target="tpu_custom_call" | custom-call | flops 4026531840 | bytes 15728640 | tf_op jit(solution)/shard_map/project/pallas_call | solution.py:283
  15.6 7.4 %all-to-all-start = ((bf16[32,64,640]{2,1,0:T(8,128)(2,1)}), bf16[32,64,640]{2,1,0:T(8,128)(2,1)S(1)}, u32[]{:S(2)}, u32[]{:S(2)}) async-start(bf16[32,64,640]{2,1,0:T(8,128)(2,1)} %get-tuple-element.16), calls=%async_computation | async-start | bytes 5242880 | tf_op jit(solution)/shard_map/all_to_all | solution.py:672
  23.1 59.6 %attend.1 = bf16[4,640,128]{2,1,0:T(8,128)(2,1)} custom-call(s32[1]{0:T(128)S(6)} %copy.12.cache_len, s32[1]{0:T(128)S(6)} %copy.13.group_len, bf16[2,2560,64]{2,1,0:T(8,128)(2,1)} %get-tuple-element.14.queries_hbm, bf16[7168,640]{1,0:T(8,128)(2,1)} %bitcast.12, bf16[1024,640]{1,0:T(8,128)(2,1)} %get-tuple-element.15.fresh_rows), custom_call_target="tpu_custom_call" | custom-call | flops 40265318400 | bytes 12582912 | tf_op jit(solution)/shard_map/attend/pallas_call | solution.py:539
  82.8 0.0 all-to-all-done.received
  82.8 1.2 %dynamic-slice_bitcast_fusion = (bf16[640,128]{1,0:T(8,128)(2,1)S(1)}, bf16[640,128]{1,0:T(8,128)(2,1)S(1)}, bf16[640,128]{1,0:T(8,128)(2,1)S(1)}, bf16[640,128]{1,0:T(8,128)(2,1)S(1)}) fusion(bf16[4,640,128]{2,1,0:T(8,128)(2,1)} %attend.1, s32[]{:T(128)S(6)} %select_n.34, s32[]{:T(128)S(6)} %select_n.32, s32[]{:T(128)S(6)} %select_n.30, s32[]{:T(128)S(6)} %select_n.28), kind=kLoop, calls=%fused_computation | loop fusion | bytes 1310736 | tf_op jit(solution)/shard_map/jit(dynamic_index_in_dim)/squeeze | solution.py:678
  84.0 4.1 %collective-permute-start.2 = (bf16[640,128]{1,0:T(8,128)(2,1)S(1)}, bf16[640,128]{1,0:T(8,128)(2,1)S(1)}, u32[]{:S(2)}, u32[]{:S(2)}) collective-permute-start(bf16[640,128]{1,0:T(8,128)(2,1)S(1)} %get-tuple-element.22), channel_id=1, source_target_pairs={{0,3},{1,0},{2,1},{3,2},{4,7},{5,4},{6,5},{7,6},{8,11},{9,8},{10,9... | collective-permute-start | bytes 491528 | tf_op jit(solution)/shard_map/ppermute | solution.py:680
  88.0 0.0 collective-permute-start.1
  88.0 1.2 %collective-permute-start = (bf16[640,128]{1,0:T(8,128)(2,1)S(1)}, bf16[640,128]{1,0:T(8,128)(2,1)S(1)}, u32[]{:S(2)}, u32[]{:S(2)}) collective-permute-start(bf16[640,128]{1,0:T(8,128)(2,1)S(1)} %get-tuple-element.24), channel_id=1, source_target_pairs={{0,1},{1,2},{2,3},{3,0},{4,5},{5,6},{6,7},{7,4},{8,9},{9,10},{10,1... | collective-permute-start | bytes 491528 | tf_op jit(solution)/shard_map/ppermute | solution.py:680
  89.3 0.0 copy-start
  89.3 2.2 %copy-done = bf16[1024,2048]{1,0:T(8,128)(2,1)S(1)} copy-done((bf16[1024,2048]{1,0:T(8,128)(2,1)S(1)}, bf16[1024,2048]{1,0:T(8,128)(2,1)}, u32[]{:S(2)}) %copy-start) | copy-done | bytes 4194328
  91.4 0.0 copy-start.1
  91.5 2.5 %copy-done.1 = bf16[1280,2048]{1,0:T(8,128)(2,1)S(1)} copy-done((bf16[1280,2048]{1,0:T(8,128)(2,1)S(1)}, bf16[1280,2048]{1,0:T(8,128)(2,1)}, u32[]{:S(2)}) %copy-start.1) | copy-done | bytes 5242904
  93.9 1.9 %store_blocks.1 = (bf16[32,64,640]{2,1,0:T(8,128)(2,1)}, bf16[1280,2048]{1,0:T(8,128)(2,1)S(1)}, bf16[256,2048]{1,0:T(8,128)(2,1)S(1)}) custom-call(bf16[32,64,640]{2,1,0:T(8,128)(2,1)S(1)} %all-to-all-done.received, bf16[1280,2048]{1,0:T(8,128)(2,1)S(1)} %copy-done.1, bf16[1024,2048]{1,0:T(8,128)(2,1)S(1)} %copy-done), custom_call_target="tpu_custom_call" | custom-call | bytes 12582912 | tf_op jit(solution)/shard_map/store_blocks/pallas_call | solution.py:587
  95.8 0.0 collective-permute-done.2.rest_2_
  95.8 0.0 collective-permute-done.1.rest_1_
  95.8 0.5 collective-permute-done.rest_0_
  96.3 2.6 %finish.1 = bf16[256,2048]{1,0:T(8,128)(2,1)} custom-call(s32[1]{0:T(128)S(6)} %copy.13.group_len, bf16[640,128]{1,0:T(8,128)(2,1)S(1)} %get-tuple-element.25.own, bf16[640,128]{1,0:T(8,128)(2,1)S(1)} %collective-permute-done.rest_0_, bf16[640,128]{1,0:T(8,128)(2,1)S(1)} %collective-permute-done.1.rest_1_, ...), custom_call_target="tpu_custom_call" | custom-call | flops 1342177280 | bytes 8388608 | tf_op jit(solution)/shard_map/finish/pallas_call | solution.py:637
Async XLA Ops:
  15.6 67.1 %all-to-all-start = ((bf16[32,64,640]{2,1,0:T(8,128)(2,1)}), bf16[32,64,640]{2,1,0:T(8,128)(2,1)S(1)}, u32[]{:S(2)}, u32[]{:S(2)}) async-start(bf16[32,64,640]{2,1,0:T(8,128)(2,1)} %get-tuple-element.16), calls=%async_computation | async-start | bytes 5242880 | tf_op jit(solution)/shard_map/all_to_all | solution.py:672
  84.0 11.8 %collective-permute-start.2 = (bf16[640,128]{1,0:T(8,128)(2,1)S(1)}, bf16[640,128]{1,0:T(8,128)(2,1)S(1)}, u32[]{:S(2)}, u32[]{:S(2)}) collective-permute-start(bf16[640,128]{1,0:T(8,128)(2,1)S(1)} %get-tuple-element.22), channel_id=1, source_target_pairs={{0,3},{1,0},{2,1},{3,2},{4,7},{5,4},{6,5},{7,6},{8,11},{9,8},{10,9... | collective-permute-start | bytes 491528 | tf_op jit(solution)/shard_map/ppermute | solution.py:680
  88.0 7.8 %collective-permute-start.1 = (bf16[640,128]{1,0:T(8,128)(2,1)S(1)}, bf16[640,128]{1,0:T(8,128)(2,1)S(1)}, u32[]{:S(2)}, u32[]{:S(2)}) collective-permute-start(bf16[640,128]{1,0:T(8,128)(2,1)S(1)} %get-tuple-element.23), channel_id=1, source_target_pairs={{0,2},{1,3},{2,0},{3,1},{4,6},{5,7},{6,4},{7,5},{8,10},{9,11},{10,... | collective-permute-start | bytes 491528 | tf_op jit(solution)/shard_map/ppermute | solution.py:680
  88.0 8.3 %collective-permute-start = (bf16[640,128]{1,0:T(8,128)(2,1)S(1)}, bf16[640,128]{1,0:T(8,128)(2,1)S(1)}, u32[]{:S(2)}, u32[]{:S(2)}) collective-permute-start(bf16[640,128]{1,0:T(8,128)(2,1)S(1)} %get-tuple-element.24), channel_id=1, source_target_pairs={{0,1},{1,2},{2,3},{3,0},{4,5},{5,6},{6,7},{7,4},{8,9},{9,10},{10,1... | collective-permute-start | bytes 491528 | tf_op jit(solution)/shard_map/ppermute | solution.py:680
  89.3 2.2 %copy-start = (bf16[1024,2048]{1,0:T(8,128)(2,1)S(1)}, bf16[1024,2048]{1,0:T(8,128)(2,1)}, u32[]{:S(2)}) copy-start(bf16[1024,2048]{1,0:T(8,128)(2,1)} %hidden.1) | copy-start | bytes 12582916
  91.4 2.5 %copy-start.1 = (bf16[1280,2048]{1,0:T(8,128)(2,1)S(1)}, bf16[1280,2048]{1,0:T(8,128)(2,1)}, u32[]{:S(2)}) copy-start(bf16[1280,2048]{1,0:T(8,128)(2,1)} %w_out.1) | copy-start | bytes 15728644

commit v5 on v4

--- a/solution.py
+++ b/solution.py
@@ -22,7 +22,6 @@
 KEPT = 1 << 20
 QUERY_ROWS = 512
 QUERY_BLOCKS = NEW_TOKEN_SLOTS // QUERY_ROWS
-STACK = LOCAL * QUERY_ROWS
 KEY_ROWS = 1792
 PREPARE_ROWS = 256
 PROJECT_ROWS = 512
@@ -80,6 +79,7 @@
     queries_hbm,
     keyval_hbm,
     outgoing_hbm,
+    own_hidden,
     queries,
     keyval,
     outgoing,
@@ -198,9 +198,7 @@
             turned = rotate(raw, cos, sin) * HEAD_SIZE**-0.5
             for head in range(2 * tile, min(2 * tile + 2, LOCAL)):
                 own = turned if head % 2 == 0 else pltpu.roll(turned, HEAD_SIZE, 1)
-                queries[block, head * QUERY_ROWS : (head + 1) * QUERY_ROWS] = own[
-                    :, :HEAD_SIZE
-                ].astype(jnp.bfloat16)
+                queries[head, here] = own[:, :HEAD_SIZE].astype(jnp.bfloat16)
 
     def trim(slot, live, value):
         rows = lax.broadcasted_iota(jnp.int32, (BLOCK_ROWS, WIDTH), 0)
@@ -234,7 +232,7 @@
                 keyval.at[here], keyval_hbm.at[here], result_semaphores.at[0, block]
             ),
             pltpu.make_async_copy(
-                queries.at[block], queries_hbm.at[block], result_semaphores.at[1, block]
+                queries.at[:, here], queries_hbm.at[:, here], result_semaphores.at[1, block]
             ),
         ]
 
@@ -243,6 +241,13 @@
         norm(piece)
     for copy in weights + loads[2:]:
         copy.wait()
+    rows = own_hidden.shape[0]
+    own_store = pltpu.make_async_copy(
+        hidden.at[pl.ds(pl.multiple_of(rank * rows, rows), rows)],
+        own_hidden,
+        semaphores.at[pieces + 2],
+    )
+    own_store.start()
     mix(0)
     norm(2)
     norm(3)
@@ -264,6 +269,7 @@
             trim(slot, fresh - block * BLOCK_ROWS, rows)
             block_store(slot).start()
 
+    own_store.wait()
     for slot in range(outgoing.shape[0]):
         block_store(slot).wait()
     for block in range(total // PROJECT_ROWS):
@@ -283,14 +289,15 @@
     return pl.pallas_call(
         project_kernel,
         out_shape=(
-            jax.ShapeDtypeStruct((QUERY_BLOCKS, STACK, HEAD_SIZE), jnp.bfloat16),
+            jax.ShapeDtypeStruct((LOCAL, rows, HEAD_SIZE), jnp.bfloat16),
             jax.ShapeDtypeStruct((rows, WIDTH), jnp.bfloat16),
             jax.ShapeDtypeStruct((count, BLOCK_ROWS, WIDTH), jnp.bfloat16),
+            jax.ShapeDtypeStruct((rows // TP, model), jnp.bfloat16),
         ),
         in_specs=[scalar, scalar, scalar, far, vector, far, far, vector, far],
-        out_specs=[far, far, far],
+        out_specs=[far, far, far, far],
         scratch_shapes=[
-            pltpu.VMEM((QUERY_BLOCKS, STACK, HEAD_SIZE), jnp.bfloat16),
+            pltpu.VMEM((LOCAL, rows, HEAD_SIZE), jnp.bfloat16),
             pltpu.VMEM((rows, WIDTH), jnp.bfloat16),
             pltpu.VMEM((count, BLOCK_ROWS, WIDTH), jnp.bfloat16),
             pltpu.SMEM((count,), jnp.int32),
@@ -302,7 +309,7 @@
             pltpu.VMEM((rows, WIDTH), jnp.float32),
             pltpu.VMEM((rows, LANES), jnp.float32),
             pltpu.VMEM((rows, LANES), jnp.float32),
-            pltpu.SemaphoreType.DMA((rows // NORM_ROWS + 2,)),
+            pltpu.SemaphoreType.DMA((rows // NORM_ROWS + 3,)),
             pltpu.SemaphoreType.DMA((count,)),
             pltpu.SemaphoreType.DMA((count,)),
             pltpu.SemaphoreType.DMA((2, rows // PROJECT_ROWS)),
@@ -331,16 +338,10 @@
     queries_hbm,
     prior,
     fresh_rows,
-    heads_out,
-    queries,
-    raw_keys,
-    raw_values,
-    keys,
-    values,
-    top,
-    total,
-    semaphores,
+    *rest,
 ):
+    outs = rest[:TP]
+    heads_out, queries, raw_keys, raw_values, keys, values, top, total, semaphores = rest[TP:]
     cached, fresh, rank = cache_len[0], group_len[0], lax.axis_index("tp")
     key_start = pl.multiple_of(key_tile_start(rank) * LANES, LANES)
     value_start = pl.multiple_of(value_tile_start(rank) * LANES, LANES)
@@ -416,87 +417,95 @@
             own = jnp.where(alive, jnp.where(lanes < HEAD_SIZE, own, 1.0), 0.0)
             values[slot, here] = own.astype(jnp.bfloat16)
 
-    def score(block, head, start, rows):
+    def score(span, head, start, rows):
         which = local_kv(rank, head)
         return jnp.dot(
-            queries[block, head * QUERY_ROWS : (head + 1) * QUERY_ROWS],
+            queries[head, span],
             keys[pl.ds(pl.multiple_of(which * HEAD_SIZE, HEAD_SIZE), HEAD_SIZE), pl.ds(start, rows)],
             preferred_element_type=jnp.float32,
         )
 
-    def blend(head, start, rows, scores, masked):
-        own = slice(head * QUERY_ROWS, (head + 1) * QUERY_ROWS)
+    def blend(span, head, start, rows, scores, masked):
         if masked:
             row = lax.broadcasted_iota(jnp.int32, scores.shape, 0)
             column = lax.broadcasted_iota(jnp.int32, scores.shape, 1)
             scores = jnp.where(column <= row, scores, -1e30)
-        before = top[own]
+        before = top[head, span]
         after = jnp.maximum(before, jnp.max(scores, axis=-1, keepdims=True))
         rescale = jnp.exp(before - after)
         chances = jnp.exp(scores - jnp.tile(after, (1, rows // LANES))).astype(jnp.bfloat16)
-        top[own] = after
-        total[own] = total[own] * rescale + jnp.dot(
+        top[head, span] = after
+        total[head, span] = total[head, span] * rescale + jnp.dot(
             chances,
             values[local_kv(rank, head), pl.ds(start, rows)],
             preferred_element_type=jnp.float32,
         )
 
-    def absorb(block, start, rows, masked):
-        pending = score(block, 0, start, rows)
-        for head in range(LOCAL):
-            following = score(block, head + 1, start, rows) if head + 1 < LOCAL else None
-            blend(head, start, rows, pending, masked)
+    def absorb(span, start, rows, masked=False):
+        pieces = [
+            (head, slice(begin, begin + QUERY_ROWS))
+            for head in range(LOCAL)
+            for begin in range(span.start, span.stop, QUERY_ROWS)
+        ]
+        pending = score(pieces[0][1], pieces[0][0], start, rows)
+        for index, (head, piece) in enumerate(pieces):
+            following = None
+            if index + 1 < len(pieces):
+                following = score(pieces[index + 1][1], pieces[index + 1][0], start, rows)
+            blend(piece, head, start, rows, pending, masked)
             pending = following
 
+    lower, upper = slice(0, QUERY_ROWS), slice(QUERY_ROWS, 2 * QUERY_ROWS)
+    everything = slice(0, 2 * QUERY_ROWS)
+    top[...] = jnp.full_like(top, -1e30)
+    total[...] = jnp.zeros_like(total)
+    for copy in fresh_copies:
+        copy.wait()
+
+    def prepare_fresh(step, inner):
+        start = pl.multiple_of(PRIOR_SLOTS + step * PREPARE_ROWS, PREPARE_ROWS)
+        prepare(start, PREPARE_ROWS)
+        return inner
+
+    lax.fori_loop(0, NEW_TOKEN_SLOTS // PREPARE_ROWS, prepare_fresh, 0)
+    absorb(lower, PRIOR_SLOTS, QUERY_ROWS, True)
+
+    @pl.when(blocks > 1)
+    def _():
+        absorb(upper, PRIOR_SLOTS, QUERY_ROWS)
+        absorb(upper, PRIOR_SLOTS + QUERY_ROWS, QUERY_ROWS, True)
+
+    def cache(step, carry):
+        start = pl.multiple_of(step * KEY_ROWS, KEY_ROWS)
+        for copy in copies(step):
+            copy.wait()
+
+        def each(part, most):
+            here = pl.multiple_of(start + part * PREPARE_ROWS, PREPARE_ROWS)
+            prepare(here, cached - here)
+            return most
+
+        lax.fori_loop(0, KEY_ROWS // PREPARE_ROWS, each, 0)
+
+        @pl.when(blocks > 1)
+        def _():
+            absorb(everything, start, KEY_ROWS)
+
+        @pl.when(blocks <= 1)
+        def _():
+            absorb(lower, start, KEY_ROWS)
+
+        return carry
+
+    lax.fori_loop(0, prior_chunks, cache, 0)
+
     def query_block(block, carry):
-        top[...] = jnp.full_like(top, -1e30)
-        total[...] = jnp.zeros_like(total)
-
-        @pl.when(block == 0)
-        def _():
-            for copy in fresh_copies:
-                copy.wait()
-
-            def each(step, inner):
-                start = pl.multiple_of(PRIOR_SLOTS + step * PREPARE_ROWS, PREPARE_ROWS)
-                prepare(start, PREPARE_ROWS)
-                return inner
-
-            lax.fori_loop(0, NEW_TOKEN_SLOTS // PREPARE_ROWS, each, 0)
-
-        def earlier(step, inner):
-            start = pl.multiple_of(PRIOR_SLOTS + step * QUERY_ROWS, QUERY_ROWS)
-            absorb(block, start, QUERY_ROWS, False)
-            return inner
-
-        def cache(step, inner):
-            start = pl.multiple_of(step * KEY_ROWS, KEY_ROWS)
-
-            @pl.when(block == 0)
-            def _():
-                for copy in copies(step):
-                    copy.wait()
-
-                def each(part, most):
-                    here = pl.multiple_of(start + part * PREPARE_ROWS, PREPARE_ROWS)
-                    prepare(here, cached - here)
-                    return most
-
-                lax.fori_loop(0, KEY_ROWS // PREPARE_ROWS, each, 0)
-
-            absorb(block, start, KEY_ROWS, False)
-            return inner
-
-        start = pl.multiple_of(PRIOR_SLOTS + block * QUERY_ROWS, QUERY_ROWS)
-        absorb(block, start, QUERY_ROWS, True)
-        lax.fori_loop(0, block, earlier, 0)
-        lax.fori_loop(0, prior_chunks, cache, 0)
-
+        here = pl.ds(pl.multiple_of(block * QUERY_ROWS, QUERY_ROWS), QUERY_ROWS)
         lanes = lane_ids(QUERY_ROWS)
         odd = rank % 2 == 1
         plain, turned = [], []
         for head in range(LOCAL):
-            sums = total[head * QUERY_ROWS : (head + 1) * QUERY_ROWS]
+            sums = total[head, here]
             swapped = pltpu.roll(sums, HEAD_SIZE, 1)
             plain.append(sums / swapped)
             turned.append(swapped / sums)
@@ -506,7 +515,7 @@
         single_turned = jnp.where(odd, turned[0], turned[4])
         near = (lane_ids(LANES) < HEAD_SIZE) != odd
         for part in range(QUERY_ROWS // PART_ROWS):
-            slot = block * (QUERY_ROWS // PART_ROWS) + part
+            slot = (block * (QUERY_ROWS // PART_ROWS) + part + TP - rank) & (TP - 1)
             rows = slice(part * PART_ROWS, (part + 1) * PART_ROWS)
             for tile in range(2):
                 pair = jnp.where(odd, odd_pairs[tile][rows], even_pairs[tile][rows])
@@ -525,12 +534,14 @@
 
     lax.fori_loop(0, blocks, query_block, 0)
 
-    def idle(slot, carry):
-        heads_out[slot] = jnp.zeros((PACKED, LANES), jnp.bfloat16)
+    def idle(part, carry):
+        heads_out[(part + TP - rank) & (TP - 1)] = jnp.zeros((PACKED, LANES), jnp.bfloat16)
         return carry
 
     parts = QUERY_ROWS // PART_ROWS
     lax.fori_loop(blocks * parts, QUERY_BLOCKS * parts, idle, 0)
+    for shift, out in enumerate(outs):
+        out[...] = heads_out[shift]
 
 
 def attend(cache_len, group_len, queries, prior, fresh_rows):
@@ -538,9 +549,7 @@
     vector = pl.BlockSpec(memory_space=pltpu.VMEM)
     return pl.pallas_call(
         attend_kernel,
-        out_shape=jax.ShapeDtypeStruct(
-            (NEW_TOKEN_SLOTS // PART_ROWS, PACKED, LANES), jnp.bfloat16
-        ),
+        out_shape=[jax.ShapeDtypeStruct((PACKED, LANES), jnp.bfloat16)] * TP,
         in_specs=[
             pl.BlockSpec(memory_space=pltpu.SMEM),
             pl.BlockSpec(memory_space=pltpu.SMEM),
@@ -548,15 +557,16 @@
             pl.BlockSpec(memory_space=pltpu.HBM),
             pl.BlockSpec(memory_space=pl.ANY),
         ],
-        out_specs=vector,
+        out_specs=[vector] * TP,
         scratch_shapes=[
+            pltpu.VMEM((TP, PACKED, LANES), jnp.bfloat16),
             pltpu.VMEM(queries.shape, queries.dtype),
             pltpu.VMEM((context, WINDOW), jnp.bfloat16),
             pltpu.VMEM((context, WINDOW), jnp.bfloat16),
             pltpu.VMEM((LANES, context), jnp.bfloat16),
             pltpu.VMEM((2, context, LANES), jnp.bfloat16),
-            pltpu.VMEM((STACK, LANES), jnp.float32),
-            pltpu.VMEM((STACK, LANES), jnp.float32),
+            pltpu.VMEM((LOCAL, NEW_TOKEN_SLOTS, LANES), jnp.float32),
+            pltpu.VMEM((LOCAL, NEW_TOKEN_SLOTS, LANES), jnp.float32),
             pltpu.SemaphoreType.DMA((2, PRIOR_SLOTS // KEY_ROWS + 2)),
         ],
         compiler_params=pltpu.CompilerParams(vmem_limit_bytes=56 * MIB),
@@ -567,13 +577,10 @@
     )(cache_len, group_len, queries, prior, fresh_rows)
 
 
-def store_kernel(received, w_out, hidden, decode, w_near, hidden_near, semaphores):
-    rows = hidden_near.shape[0]
-    begin = pl.multiple_of(lax.axis_index("tp") * rows, rows)
+def store_kernel(received, w_out, decode, w_near, semaphores):
     copies = (
         pltpu.make_async_copy(w_out, w_near, semaphores.at[0]),
         pltpu.make_async_copy(received, decode, semaphores.at[1]),
-        pltpu.make_async_copy(hidden.at[pl.ds(begin, rows)], hidden_near, semaphores.at[2]),
     )
     for copy in copies:
         copy.start()
@@ -581,7 +588,7 @@
         copy.wait()
 
 
-def store_blocks(received, w_out, hidden_in):
+def store_blocks(received, w_out):
     vector = pl.BlockSpec(memory_space=pltpu.VMEM)
     far = pl.BlockSpec(memory_space=pltpu.HBM)
     return pl.pallas_call(
@@ -589,15 +596,14 @@
         out_shape=(
             jax.ShapeDtypeStruct(received.shape, received.dtype),
             jax.ShapeDtypeStruct(w_out.shape, w_out.dtype),
-            jax.ShapeDtypeStruct((PART_ROWS, hidden_in.shape[1]), hidden_in.dtype),
         ),
-        in_specs=[vector, far, far],
-        out_specs=[far, vector, vector],
-        scratch_shapes=[pltpu.SemaphoreType.DMA((3,))],
+        in_specs=[vector, far],
+        out_specs=[far, vector],
+        scratch_shapes=[pltpu.SemaphoreType.DMA((2,))],
         compiler_params=pltpu.CompilerParams(vmem_limit_bytes=STORE_LIMIT * MIB),
         cost_estimate=pl.CostEstimate(flops=0, bytes_accessed=12 * MIB, transcendentals=0),
         name="store_blocks",
-    )(received, w_out, hidden_in)
+    )(received, w_out)
 
 
 def finish_kernel(group_len, own, *rest):
@@ -665,21 +671,19 @@
     page_map,
 ):
     prior = prior_cache[0]
-    queries, keyval, outgoing = project(
+    queries, keyval, outgoing, own_hidden = project(
         cache_len, group_len, page_map, hidden_in, norm_gain, w_query, key_value_weight, prior
     )
     outgoing, queries = lax.optimization_barrier((outgoing, queries))
     received = lax.all_to_all(outgoing, "req", split_axis=0, concat_axis=0, tiled=True)
     attended = attend(cache_len, group_len, queries, prior, keyval)
     attended, received = lax.optimization_barrier((attended, received))
-    rank = lax.axis_index("tp")
-    heads = [lax.dynamic_index_in_dim(attended, rank, 0, keepdims=False)]
+    heads = [attended[0]]
     for shift in range(1, TP):
-        part = lax.dynamic_index_in_dim(attended, (rank + shift) % TP, 0, keepdims=False)
         pairs = [(source, (source + shift) % TP) for source in range(TP)]
-        heads.append(lax.ppermute(part, "tp", pairs))
-    decode_kv, w_near, hidden_near = store_blocks(received, w_out, hidden_in)
-    hidden_out = finish(group_len, heads, w_near, hidden_near)
+        heads.append(lax.ppermute(attended[shift], "tp", pairs))
+    decode_kv, w_near = store_blocks(received, w_out)
+    hidden_out = finish(group_len, heads, w_near, own_hidden)
     return (hidden_out, decode_kv[None])
 
 

time: 101 us -> 96.7 us (0.957)
  the two profiles are of different devices: /device:TPU:24 before, /device:TPU:15 now
where the time goes in v5:
time: 96.7 us; the launch traced here: 97.2 us
  Pallas kernels  76.6 us (79%)
  starting transfers between devices  13.6 us (14%)
  waiting for transfers between devices  2.49 us (3%)
  local copies, waits for them, and re-layouts  2.49 us (3%)
  between operations  1.98 us (2%)
    pallas_call x1, Pallas kernels, attend(): pl.pallas_call(attend_kernel, out_shape=[jax.ShapeDtypeStruct((PACKED, LA...  58.3 us
    pallas_call x1, Pallas kernels, project(): pl.pallas_call(project_kernel, out_shape=(jax.ShapeDtypeStruct((LOCAL, ro...  13.9 us
    all_to_all x1, starting transfers between devices, shards(): lax.all_to_all(outgoing, 'req', split_axis=0, concat_axis=0, tiled=True)  7.81 us
    ppermute x3, starting transfers between devices, shards(): heads.append(lax.ppermute(attended[shift], 'tp', pairs))  5.77 us
    pallas_call x1, Pallas kernels, finish(): pl.pallas_call(finish_kernel, out_shape=jax.ShapeDtypeStruct((PART_ROWS,...  2.64 us
    unnamed x6, local copies, waits for them, and re-layouts  2.49 us
    ppermute x3, waiting for transfers between devices, shards(): heads.append(lax.ppermute(attended[shift], 'tp', pairs))  2.48 us
  transfers between devices with their start and end apart: 4, of which 1 were waited for; matrix products, arithmetic and copies ran while one was open for 0% of the time, Pallas kernels for 62%

profile of v5, /device:TPU:15, one launch (start us, length us, event | category | flops | bytes accessed | tf_op | source)
XLA Modules:
  0.0 97.2 jit_solution(2530487343532068030)
XLA Ops:
  1.9 13.9 %project.1 = (bf16[5,1024,64]{2,1,0:T(8,128)(2,1)}, bf16[1024,640]{1,0:T(8,128)(2,1)}, bf16[32,64,640]{2,1,0:T(8,128)(2,1)}, bf16[256,2048]{1,0:T(8,128)(2,1)}) custom-call(s32[1]{0:T(128)S(6)} %copy.12.cache_len, s32[1]{0:T(128)S(6)} %copy.13.group_len, s32[1,128]{1,0:T(1,128)} %page_map.1, bf16[1024,2048]{1,0:T(8,128)(2,1)} %hidden_hbm.1, ...), custom_call_target="tpu_custom_call" | custom-call | flops 4026531840 | bytes 15728640 | tf_op jit(solution)/shard_map/project/pallas_call | solution.py:289
  15.8 7.8 %all-to-all-start = ((bf16[32,64,640]{2,1,0:T(8,128)(2,1)}), bf16[32,64,640]{2,1,0:T(8,128)(2,1)S(1)}, u32[]{:S(2)}, u32[]{:S(2)}) async-start(bf16[32,64,640]{2,1,0:T(8,128)(2,1)} %get-tuple-element.27), calls=%async_computation | async-start | bytes 5242880 | tf_op jit(solution)/shard_map/all_to_all | solution.py:678
  23.6 58.3 %attend.1 = (bf16[640,128]{1,0:T(8,128)(2,1)}, bf16[640,128]{1,0:T(8,128)(2,1)}, bf16[640,128]{1,0:T(8,128)(2,1)}, bf16[640,128]{1,0:T(8,128)(2,1)}) custom-call(s32[1]{0:T(128)S(6)} %copy.12.cache_len, s32[1]{0:T(128)S(6)} %copy.13.group_len, bf16[5,1024,64]{2,1,0:T(8,128)(2,1)} %get-tuple-element.21.queries_hbm, bf16[7168,640]{1,0:T(8,128)(2,1)} %bitcast.4, ...), custom_call_target="tpu_custom_call" | custom-call | flops 40265318400 | bytes 12582912 | tf_op jit(solution)/shard_map/attend/pallas_call | solution.py:550
  81.9 0.0 all-to-all-done.received
  81.9 1.6 %collective-permute-start = (bf16[640,128]{1,0:T(8,128)(2,1)}, bf16[640,128]{1,0:T(8,128)(2,1)S(1)}, u32[]{:S(2)}, u32[]{:S(2)}) collective-permute-start(bf16[640,128]{1,0:T(8,128)(2,1)} %get-tuple-element.29), channel_id=1, source_target_pairs={{0,1},{1,2},{2,3},{3,0},{4,5},{5,6},{6,7},{7,4},{8,9},{9,10},{10,1... | collective-permute-start | bytes 491528 | tf_op jit(solution)/shard_map/ppermute | solution.py:684
  83.5 3.3 %collective-permute-start.1 = (bf16[640,128]{1,0:T(8,128)(2,1)}, bf16[640,128]{1,0:T(8,128)(2,1)S(1)}, u32[]{:S(2)}, u32[]{:S(2)}) collective-permute-start(bf16[640,128]{1,0:T(8,128)(2,1)} %get-tuple-element.30), channel_id=1, source_target_pairs={{0,2},{1,3},{2,0},{3,1},{4,6},{5,7},{6,4},{7,5},{8,10},{9,11},{10,... | collective-permute-start | bytes 491528 | tf_op jit(solution)/shard_map/ppermute | solution.py:684
  86.8 0.8 collective-permute-start.2
  87.7 0.0 copy-start
  87.7 2.5 %copy-done = bf16[1280,2048]{1,0:T(8,128)(2,1)S(1)} copy-done((bf16[1280,2048]{1,0:T(8,128)(2,1)S(1)}, bf16[1280,2048]{1,0:T(8,128)(2,1)}, u32[]{:S(2)}) %copy-start) | copy-done | bytes 5242904
  90.2 0.0 copy-start.1
  90.2 0.0 copy-start.2
  90.2 1.9 %store_blocks.1 = (bf16[32,64,640]{2,1,0:T(8,128)(2,1)}, bf16[1280,2048]{1,0:T(8,128)(2,1)S(1)}) custom-call(bf16[32,64,640]{2,1,0:T(8,128)(2,1)S(1)} %all-to-all-done.received, bf16[1280,2048]{1,0:T(8,128)(2,1)S(1)} %copy-done), custom_call_target="tpu_custom_call" | custom-call | bytes 12582912 | tf_op jit(solution)/shard_map/store_blocks/pallas_call | solution.py:594
  92.0 0.0 collective-permute-done.rest_0_
  92.0 2.5 %collective-permute-done.1.rest_1_ = bf16[640,128]{1,0:T(8,128)(2,1)S(1)} collective-permute-done((bf16[640,128]{1,0:T(8,128)(2,1)}, bf16[640,128]{1,0:T(8,128)(2,1)S(1)}, u32[]{:S(2)}, u32[]{:S(2)}) %collective-permute-start.1) | collective-permute-done | bytes 163872 | tf_op jit(solution)/shard_map/ppermute | solution.py:684
  94.5 0.0 collective-permute-done.2.rest_2_
  94.5 0.0 copy-done.1
  94.5 0.0 copy-done.2
  94.5 2.6 %finish.1 = bf16[256,2048]{1,0:T(8,128)(2,1)} custom-call(s32[1]{0:T(128)S(6)} %copy.13.group_len, bf16[640,128]{1,0:T(8,128)(2,1)S(1)} %copy-done.2, bf16[640,128]{1,0:T(8,128)(2,1)S(1)} %collective-permute-done.rest_0_, bf16[640,128]{1,0:T(8,128)(2,1)S(1)} %collective-permute-done.1.rest_1_, bf16[640,128]{1,0:T(8,128)(2,1)S(1)} %collective-permute-done.2.rest_2_, ...), custom_call_target="tpu_custom_call" | custom-call | flops 1342177280 | bytes 8388608 | tf_op jit(solution)/shard_map/finish/pallas_call | solution.py:643
Async XLA Ops:
  15.8 66.1 %all-to-all-start = ((bf16[32,64,640]{2,1,0:T(8,128)(2,1)}), bf16[32,64,640]{2,1,0:T(8,128)(2,1)S(1)}, u32[]{:S(2)}, u32[]{:S(2)}) async-start(bf16[32,64,640]{2,1,0:T(8,128)(2,1)} %get-tuple-element.27), calls=%async_computation | async-start | bytes 5242880 | tf_op jit(solution)/shard_map/all_to_all | solution.py:678
  81.9 10.1 %collective-permute-start = (bf16[640,128]{1,0:T(8,128)(2,1)}, bf16[640,128]{1,0:T(8,128)(2,1)S(1)}, u32[]{:S(2)}, u32[]{:S(2)}) collective-permute-start(bf16[640,128]{1,0:T(8,128)(2,1)} %get-tuple-element.29), channel_id=1, source_target_pairs={{0,1},{1,2},{2,3},{3,0},{4,5},{5,6},{6,7},{7,4},{8,9},{9,10},{10,1... | collective-permute-start | bytes 491528 | tf_op jit(solution)/shard_map/ppermute | solution.py:684
  83.5 11.0 %collective-permute-start.1 = (bf16[640,128]{1,0:T(8,128)(2,1)}, bf16[640,128]{1,0:T(8,128)(2,1)S(1)}, u32[]{:S(2)}, u32[]{:S(2)}) collective-permute-start(bf16[640,128]{1,0:T(8,128)(2,1)} %get-tuple-element.30), channel_id=1, source_target_pairs={{0,2},{1,3},{2,0},{3,1},{4,6},{5,7},{6,4},{7,5},{8,10},{9,11},{10,... | collective-permute-start | bytes 491528 | tf_op jit(solution)/shard_map/ppermute | solution.py:684
  86.8 7.7 %collective-permute-start.2 = (bf16[640,128]{1,0:T(8,128)(2,1)}, bf16[640,128]{1,0:T(8,128)(2,1)S(1)}, u32[]{:S(2)}, u32[]{:S(2)}) collective-permute-start(bf16[640,128]{1,0:T(8,128)(2,1)} %get-tuple-element.31), channel_id=1, source_target_pairs={{0,3},{1,0},{2,1},{3,2},{4,7},{5,4},{6,5},{7,6},{8,11},{9,8},{10,9... | collective-permute-start | bytes 491528 | tf_op jit(solution)/shard_map/ppermute | solution.py:684
  87.7 2.5 %copy-start = (bf16[1280,2048]{1,0:T(8,128)(2,1)S(1)}, bf16[1280,2048]{1,0:T(8,128)(2,1)}, u32[]{:S(2)}) copy-start(bf16[1280,2048]{1,0:T(8,128)(2,1)} %w_out.1) | copy-start | bytes 15728644
  90.2 4.4 %copy-start.1 = (bf16[256,2048]{1,0:T(8,128)(2,1)S(1)}, bf16[256,2048]{1,0:T(8,128)(2,1)}, u32[]{:S(2)}) copy-start(bf16[256,2048]{1,0:T(8,128)(2,1)} %get-tuple-element.34.rest_4_) | copy-start | bytes 3145732
  90.2 4.4 %copy-start.2 = (bf16[640,128]{1,0:T(8,128)(2,1)S(1)}, bf16[640,128]{1,0:T(8,128)(2,1)}, u32[]{:S(2)}) copy-start(bf16[640,128]{1,0:T(8,128)(2,1)} %get-tuple-element.28.own) | copy-start | bytes 491524
